TPU v7x, 32 devices: a whole 2x2x4 slice. The times are simulated.
32 devices in a mesh: dp: 4 (over y, core), row: 2 (over x), col: 4 (over z).
Axes of the slice: x: 2, y: 2, z: 4, core: 2. Of those that a mesh axis runs over, the one named last changes fastest.
Arguments:
- tokens: float32 [16384, 1024], P(('dp', 'row', 'col')), may hold values from -6 to 6
- segment_ids: int32 [16384], P(('dp', 'row', 'col')), may hold values from 0 to 127, never falling along the last dimension, each value on 1 to 512 neighbouring positions
- cotangent: float32 [16384, 1024], P(('dp', 'row', 'col')), may hold values from -6 to 6
- weight_query: float32 [1024, 1024], P('row', 'col'), as said below
- weight_key: float32 [1024, 1024], P('row', 'col'), may hold values from -0.1875 to 0.1875
- weight_value: float32 [1024, 1024], P('row', 'col'), may hold values from -0.1875 to 0.1875
- weight_output: float32 [1024, 1024], P('row', 'col'), may hold values from -0.75 to 0.75
- weight_inner: float32 [1024, 4096], P('row', 'col'), may hold values from -0.1875 to 0.1875
- weight_outer: float32 [4096, 1024], P('row', 'col'), may hold values from -0.09375 to 0.09375
- bias_query: float32 [1024], P(('row', 'col')), may hold values from -1.5 to 1.5
- bias_value: float32 [1024], P(('row', 'col')), may hold values from -1.5 to 1.5
- bias_output: float32 [1024], P(('row', 'col')), may hold values from -1.5 to 1.5
- bias_inner: float32 [4096], P(('row', 'col')), may hold values from -1.5 to 1.5
- bias_outer: float32 [1024], P(('row', 'col')), may hold values from -1.5 to 1.5
- gain_attn: float32 [1024], P(('row', 'col')), may hold values from 0.25 to 1.75
- shift_attn: float32 [1024], P(('row', 'col')), may hold values from -1.5 to 1.5
- gain_block: float32 [1024], P(('row', 'col')), may hold values from 0.25 to 1.75
- shift_block: float32 [1024], P(('row', 'col')), may hold values from -1.5 to 1.5
- tau_num: int32 [1], replicated, may hold values from 100 to 399
- tau_den: int32 [1], replicated, may hold values from 400 to 999
Outputs:
- output: float32 [16384, 1024], P(('dp', 'row', 'col'))
- grad_tokens: float32 [16384, 1024], P(('dp', 'row', 'col'))
- grad_weight_query: float32 [1024, 1024], P('row', 'col')
- grad_weight_key: float32 [1024, 1024], P('row', 'col')
- grad_weight_value: float32 [1024, 1024], P('row', 'col')
- grad_weight_output: float32 [1024, 1024], P('row', 'col')
- grad_weight_inner: float32 [1024, 4096], P('row', 'col')
- grad_weight_outer: float32 [4096, 1024], P('row', 'col')
- grad_bias_query: float32 [1024], P(('row', 'col'))
- grad_bias_value: float32 [1024], P(('row', 'col'))
- grad_bias_output: float32 [1024], P(('row', 'col'))
- grad_bias_inner: float32 [4096], P(('row', 'col'))
- grad_bias_outer: float32 [1024], P(('row', 'col'))
- grad_gain_attn: float32 [1024], P(('row', 'col'))
- grad_shift_attn: float32 [1024], P(('row', 'col'))
- grad_gain_block: float32 [1024], P(('row', 'col'))
- grad_shift_block: float32 [1024], P(('row', 'col'))
- head_peak: float32 [16], replicated
- clipped_query: float32 [1024, 1024], P('row', 'col')
- clipped_key: float32 [1024, 1024], P('row', 'col')
Inputs may be any that keep to these rules, and one draw needn't show every extreme that they name: `segment_ids`: along the tokens the numbers never fall; each document covers 1 to 512 consecutive tokens, one exactly 512. `weight_query`: entries within 18 / sqrt(1024) in magnitude.
All inputs are finite; a program needn't handle non-finite values.
Results may differ from a plain program's by a relative error of at most 0.019.
The roundings to bfloat16 on the way count: a program that leaves them out, or rounds other values in their place, can miss the bound.
Values may be sent and summed in bfloat16 or wider, within the bound.
A program may use at most 256 MiB of HBM per device.

v0:
```python
import jax
import jax.numpy as jnp
from jax import lax
from jax.sharding import PartitionSpec as P

H = 16
DH = 64
SEQ = 512


norm_eps = 1e-12
neg_fill = -1e30


def norm_rows(values, gain_vec, shift_vec):
    center = values - jnp.mean(values, axis=-1, keepdims=True)
    spread = jnp.mean(center * center, axis=-1, keepdims=True)
    return center * lax.rsqrt(spread + norm_eps) * gain_vec + shift_vec


def gelu_exact(values):
    return jax.nn.gelu(values, approximate=False)


def apply_weight(operand, weight):
    row_count, col_count, rows_in, cols_out = weight.shape
    token_count = operand.shape[0]
    result = jnp.einsum(
        "trk,rckn->tcn",
        operand.reshape(token_count, row_count, rows_in),
        weight,
        preferred_element_type=jnp.float32,
    )
    return result.reshape(token_count, col_count * cols_out)


def apply_back(gradient, weight):
    row_count, col_count, rows_in, cols_out = weight.shape
    token_count = gradient.shape[0]
    result = jnp.einsum(
        "tcn,rckn->trk",
        gradient.reshape(token_count, col_count, cols_out),
        weight,
        preferred_element_type=jnp.float32,
    )
    return result.reshape(token_count, row_count * rows_in)


def weight_term(operand, gradient, row_count, col_count, pieces):
    token_count, width_in = operand.shape
    width_out = gradient.shape[1]
    piece_rows = width_in // (row_count * pieces)
    left_blocks = operand.reshape(token_count, row_count, pieces, piece_rows)
    right_blocks = gradient.reshape(token_count, col_count, width_out // col_count)
    term = jnp.einsum(
        "trdk,tcn->drckn", left_blocks, right_blocks, preferred_element_type=jnp.float32
    )
    return term.reshape(pieces * row_count * col_count, piece_rows, width_out // col_count)


def vector_term(vector, group_count, pieces):
    return (
        vector.reshape(group_count, pieces, -1).transpose(1, 0, 2).reshape(pieces * group_count, -1)
    )


def column_sum(gradient_low):
    return jnp.sum(gradient_low, axis=0, dtype=jnp.float32)


def to_wire(block):
    return block.astype(jnp.bfloat16)[None]


def unpack(gathered, row_count, col_count):
    matrices = tuple(
        (
            shard_item.reshape(row_count, col_count, shard_item.shape[1], shard_item.shape[2])
            for shard_item in gathered[:6]
        )
    )
    vectors = tuple((shard_item.reshape(-1).astype(jnp.float32) for shard_item in gathered[6:]))
    return matrices + vectors


def fetch_params(wire_items):
    return (
        lax.all_gather(wire_items[0], ("row", "col"), axis=0, tiled=True),
        lax.all_gather(wire_items[1], ("row", "col"), axis=0, tiled=True),
        lax.all_gather(wire_items[2], ("row", "col"), axis=0, tiled=True),
        lax.all_gather(wire_items[3], ("row", "col"), axis=0, tiled=True),
        lax.all_gather(wire_items[4], ("row", "col"), axis=0, tiled=True),
        lax.all_gather(wire_items[5], ("row", "col"), axis=0, tiled=True),
        lax.all_gather(wire_items[6], ("row", "col"), axis=0, tiled=True),
        lax.all_gather(wire_items[7], ("row", "col"), axis=0, tiled=True),
        lax.all_gather(wire_items[8], ("row", "col"), axis=0, tiled=True),
        lax.all_gather(wire_items[9], ("row", "col"), axis=0, tiled=True),
        lax.all_gather(wire_items[10], ("row", "col"), axis=0, tiled=True),
        lax.all_gather(wire_items[11], ("row", "col"), axis=0, tiled=True),
        lax.all_gather(wire_items[12], ("row", "col"), axis=0, tiled=True),
        lax.all_gather(wire_items[13], ("row", "col"), axis=0, tiled=True),
        lax.all_gather(wire_items[14], ("row", "col"), axis=0, tiled=True),
    )


def masked_scores(query_heads, key_heads, allowed):
    scores = jnp.einsum(
        "sqhd,skhd->shqk", query_heads, key_heads, preferred_element_type=jnp.float32
    ) * DH ** (-0.5)
    return jnp.where(allowed, scores, neg_fill)


def on_device(
    tokens,
    segment_ids,
    cotangent,
    weight_query,
    weight_key,
    weight_value,
    weight_output,
    weight_inner,
    weight_outer,
    bias_query,
    bias_value,
    bias_output,
    bias_inner,
    bias_outer,
    gain_attn,
    shift_attn,
    gain_block,
    shift_block,
    tau_num,
    tau_den,
):
    row_count = lax.axis_size("row")
    col_count = lax.axis_size("col")
    group_count = row_count * col_count
    wire_items = tuple(
        (
            to_wire(block)
            for block in (
                weight_query,
                weight_key,
                weight_value,
                weight_output,
                weight_inner,
                weight_outer,
                bias_query,
                bias_value,
                bias_output,
                bias_inner,
                bias_outer,
                gain_attn,
                shift_attn,
                gain_block,
                shift_block,
            )
        )
    )
    params_full = unpack(fetch_params(wire_items), row_count, col_count)
    (
        whole_query,
        whole_key,
        whole_value,
        whole_output,
        whole_inner,
        whole_outer,
        add_query,
        add_value,
        add_output,
        add_inner,
        add_outer,
        scale_attn,
        offset_attn,
        scale_block,
        offset_block,
    ) = params_full
    token_count = tokens.shape[0]
    seq_count = token_count // SEQ
    head_shape = (seq_count, SEQ, H, DH)
    token_low = tokens.astype(jnp.bfloat16)
    query_low = (apply_weight(token_low, whole_query) + add_query).astype(jnp.bfloat16)
    key_low = apply_weight(token_low, whole_key).astype(jnp.bfloat16)
    value_low = (apply_weight(token_low, whole_value) + add_value).astype(jnp.bfloat16)
    query_heads = query_low.reshape(head_shape)
    key_heads = key_low.reshape(head_shape)
    value_heads = value_low.reshape(head_shape)
    segment_rows = segment_ids.reshape(seq_count, SEQ)
    allowed = (segment_rows[:, :, None] == segment_rows[:, None, :])[:, None, :, :]
    masked = masked_scores(query_heads, key_heads, allowed)
    local_top = jnp.max(masked, axis=(0, 2, 3))
    row_top = jnp.max(masked, axis=-1, keepdims=True)
    raised = jnp.exp(masked - row_top)
    row_total = jnp.sum(raised, axis=-1, keepdims=True)
    attend = raised / row_total
    log_total = row_top + jnp.log(row_total)
    context = jnp.einsum(
        "shqk,skhd->sqhd",
        attend.astype(jnp.bfloat16),
        value_heads,
        preferred_element_type=jnp.float32,
    )
    context_low = context.reshape(token_count, H * DH).astype(jnp.bfloat16)
    first_sum = tokens + apply_weight(context_low, whole_output) + add_output
    normed = norm_rows(first_sum, scale_attn, offset_attn)
    normed_low = normed.astype(jnp.bfloat16)
    hidden_pre = apply_weight(normed_low, whole_inner) + add_inner
    activated_low = gelu_exact(hidden_pre).astype(jnp.bfloat16)
    second_sum = normed + apply_weight(activated_low, whole_outer) + add_outer
    output = norm_rows(second_sum, scale_block, offset_block)
    head_peak = lax.pmax(local_top, ("dp", "row", "col"))
    back_query, back_key, back_value, back_output, back_inner, back_outer = params_full[:6]
    grad_second, grad_scale_block, grad_offset_block = jax.vjp(
        norm_rows, second_sum, scale_block, offset_block
    )[1](cotangent)
    outer_grad_low = grad_second.astype(jnp.bfloat16)
    act_grad = apply_back(outer_grad_low, back_outer)
    hidden_grad_low = jax.vjp(gelu_exact, hidden_pre)[1](act_grad)[0].astype(jnp.bfloat16)
    normed_grad = grad_second + apply_back(hidden_grad_low, back_inner)
    grad_first, grad_scale_attn, grad_offset_attn = jax.vjp(
        norm_rows, first_sum, scale_attn, offset_attn
    )[1](normed_grad)
    branch_grad_low = grad_first.astype(jnp.bfloat16)
    context_grad_low = apply_back(branch_grad_low, back_output).astype(jnp.bfloat16)
    masked_again = masked_scores(query_heads, key_heads, allowed)
    attend_again = jnp.exp(masked_again - log_total)
    attend_low = attend_again.astype(jnp.bfloat16)
    context_grad_heads = context_grad_low.reshape(head_shape)
    value_grad = jnp.einsum(
        "shqk,sqhd->skhd", attend_low, context_grad_heads, preferred_element_type=jnp.float32
    )
    attend_grad = jnp.einsum(
        "sqhd,skhd->shqk", context_grad_heads, value_heads, preferred_element_type=jnp.float32
    )
    score_grad = attend_again * (
        attend_grad - jnp.sum(attend_again * attend_grad, axis=-1, keepdims=True)
    )
    score_grad_low = score_grad.astype(jnp.bfloat16)
    query_grad = jnp.einsum(
        "shqk,skhd->sqhd", score_grad_low, key_heads, preferred_element_type=jnp.float32
    ) * DH ** (-0.5)
    key_grad = jnp.einsum(
        "shqk,sqhd->skhd", score_grad_low, query_heads, preferred_element_type=jnp.float32
    ) * DH ** (-0.5)
    query_grad_low = query_grad.reshape(token_count, H * DH).astype(jnp.bfloat16)
    key_grad_low = key_grad.reshape(token_count, H * DH).astype(jnp.bfloat16)
    value_grad_low = value_grad.reshape(token_count, H * DH).astype(jnp.bfloat16)
    grad_tokens = (
        grad_first
        + apply_back(query_grad_low, back_query)
        + apply_back(key_grad_low, back_key)
        + apply_back(value_grad_low, back_value)
    )
    pieces = 1
    terms = (
        weight_term(token_low, query_grad_low, row_count, col_count, pieces),
        weight_term(token_low, key_grad_low, row_count, col_count, pieces),
        weight_term(token_low, value_grad_low, row_count, col_count, pieces),
        weight_term(context_low, branch_grad_low, row_count, col_count, pieces),
        weight_term(normed_low, hidden_grad_low, row_count, col_count, pieces),
        weight_term(activated_low, outer_grad_low, row_count, col_count, pieces),
        vector_term(column_sum(query_grad_low), group_count, pieces),
        vector_term(column_sum(value_grad_low), group_count, pieces),
        vector_term(column_sum(branch_grad_low), group_count, pieces),
        vector_term(column_sum(hidden_grad_low), group_count, pieces),
        vector_term(column_sum(outer_grad_low), group_count, pieces),
        vector_term(grad_scale_attn, group_count, pieces),
        vector_term(grad_offset_attn, group_count, pieces),
        vector_term(grad_scale_block, group_count, pieces),
        vector_term(grad_offset_block, group_count, pieces),
    )
    parted = (
        lax.psum_scatter(
            terms[0].astype(jnp.bfloat16), ("row", "col"), scatter_dimension=0, tiled=True
        ).astype(jnp.float32),
        lax.psum_scatter(
            terms[1].astype(jnp.bfloat16), ("row", "col"), scatter_dimension=0, tiled=True
        ).astype(jnp.float32),
        lax.psum_scatter(
            terms[2].astype(jnp.bfloat16), ("row", "col"), scatter_dimension=0, tiled=True
        ).astype(jnp.float32),
        lax.psum_scatter(
            terms[3].astype(jnp.bfloat16), ("row", "col"), scatter_dimension=0, tiled=True
        ).astype(jnp.float32),
        lax.psum_scatter(
            terms[4].astype(jnp.bfloat16), ("row", "col"), scatter_dimension=0, tiled=True
        ).astype(jnp.float32),
        lax.psum_scatter(
            terms[5].astype(jnp.bfloat16), ("row", "col"), scatter_dimension=0, tiled=True
        ).astype(jnp.float32),
        lax.psum_scatter(
            terms[6].astype(jnp.bfloat16), ("row", "col"), scatter_dimension=0, tiled=True
        ).astype(jnp.float32),
        lax.psum_scatter(
            terms[7].astype(jnp.bfloat16), ("row", "col"), scatter_dimension=0, tiled=True
        ).astype(jnp.float32),
        lax.psum_scatter(
            terms[8].astype(jnp.bfloat16), ("row", "col"), scatter_dimension=0, tiled=True
        ).astype(jnp.float32),
        lax.psum_scatter(
            terms[9].astype(jnp.bfloat16), ("row", "col"), scatter_dimension=0, tiled=True
        ).astype(jnp.float32),
        lax.psum_scatter(
            terms[10].astype(jnp.bfloat16), ("row", "col"), scatter_dimension=0, tiled=True
        ).astype(jnp.float32),
        lax.psum_scatter(
            terms[11].astype(jnp.bfloat16), ("row", "col"), scatter_dimension=0, tiled=True
        ).astype(jnp.float32),
        lax.psum_scatter(
            terms[12].astype(jnp.bfloat16), ("row", "col"), scatter_dimension=0, tiled=True
        ).astype(jnp.float32),
        lax.psum_scatter(
            terms[13].astype(jnp.bfloat16), ("row", "col"), scatter_dimension=0, tiled=True
        ).astype(jnp.float32),
        lax.psum_scatter(
            terms[14].astype(jnp.bfloat16), ("row", "col"), scatter_dimension=0, tiled=True
        ).astype(jnp.float32),
    )
    summed = (
        lax.psum(parted[0][0].astype(jnp.bfloat16), "dp").astype(jnp.float32),
        lax.psum(parted[1][0].astype(jnp.bfloat16), "dp").astype(jnp.float32),
        lax.psum(parted[2][0].astype(jnp.bfloat16), "dp").astype(jnp.float32),
        lax.psum(parted[3][0].astype(jnp.bfloat16), "dp").astype(jnp.float32),
        lax.psum(parted[4][0].astype(jnp.bfloat16), "dp").astype(jnp.float32),
        lax.psum(parted[5][0].astype(jnp.bfloat16), "dp").astype(jnp.float32),
        lax.psum(parted[6][0].astype(jnp.bfloat16), "dp").astype(jnp.float32),
        lax.psum(parted[7][0].astype(jnp.bfloat16), "dp").astype(jnp.float32),
        lax.psum(parted[8][0].astype(jnp.bfloat16), "dp").astype(jnp.float32),
        lax.psum(parted[9][0].astype(jnp.bfloat16), "dp").astype(jnp.float32),
        lax.psum(parted[10][0].astype(jnp.bfloat16), "dp").astype(jnp.float32),
        lax.psum(parted[11][0].astype(jnp.bfloat16), "dp").astype(jnp.float32),
        lax.psum(parted[12][0].astype(jnp.bfloat16), "dp").astype(jnp.float32),
        lax.psum(parted[13][0].astype(jnp.bfloat16), "dp").astype(jnp.float32),
        lax.psum(parted[14][0].astype(jnp.bfloat16), "dp").astype(jnp.float32),
    )
    tau_value = tau_num[0].astype(jnp.float32) / tau_den[0].astype(jnp.float32)
    factor = jnp.sqrt(tau_value / jnp.maximum(head_peak, tau_value))
    col_width = weight_query.shape[1]
    col_heads = (lax.axis_index("col") * col_width + jnp.arange(col_width, dtype=jnp.int32)) // DH
    column_factor = jnp.sum(
        jnp.where(
            col_heads[:, None] == jnp.arange(H, dtype=jnp.int32)[None, :], factor[None, :], 0.0
        ),
        axis=1,
    )
    return (
        output,
        grad_tokens,
        summed[0],
        summed[1],
        summed[2],
        summed[3],
        summed[4],
        summed[5],
        summed[6],
        summed[7],
        summed[8],
        summed[9],
        summed[10],
        summed[11],
        summed[12],
        summed[13],
        summed[14],
        head_peak,
        weight_query * column_factor[None, :],
        weight_key * column_factor[None, :],
    )


def solution(mesh):
    in_specs = (
        P(("dp", "row", "col"), None),
        P(("dp", "row", "col")),
        P(("dp", "row", "col"), None),
        P("row", "col"),
        P("row", "col"),
        P("row", "col"),
        P("row", "col"),
        P("row", "col"),
        P("row", "col"),
        P(("row", "col")),
        P(("row", "col")),
        P(("row", "col")),
        P(("row", "col")),
        P(("row", "col")),
        P(("row", "col")),
        P(("row", "col")),
        P(("row", "col")),
        P(("row", "col")),
        P(),
        P(),
    )
    out_specs = (
        P(("dp", "row", "col"), None),
        P(("dp", "row", "col"), None),
        P("row", "col"),
        P("row", "col"),
        P("row", "col"),
        P("row", "col"),
        P("row", "col"),
        P("row", "col"),
        P(("row", "col")),
        P(("row", "col")),
        P(("row", "col")),
        P(("row", "col")),
        P(("row", "col")),
        P(("row", "col")),
        P(("row", "col")),
        P(("row", "col")),
        P(("row", "col")),
        P(),
        P("row", "col"),
        P("row", "col"),
    )
    return jax.shard_map(
        on_device, mesh=mesh, in_specs=in_specs, out_specs=out_specs, check_vma=False
    )
```

profile of v0, /device:TPU:5, one launch (start us, length us, event | category | flops | bytes accessed | tf_op | source)
XLA Modules:
  0.0 1223.0 jit_solution(10910382905271209997)
XLA Ops:
  19.2 17.1 %all-gather.16 = bf16[8,1,128]{2,1,0:T(2,128)(2,1)S(1)} all-gather(bf16[1,1,128]{2,1,0:T(2,128)(2,1)S(1)} %convert_bitcast_fusion.16), channel_id=5, replica_groups=mesh['dp'=4,'row'=2,'col'=4] {'row','col'}, dimensions={0}, use_global_device_ids=true | all-gather | bytes 2304 | tf_op jit(solution)/shard_map/all_gather | solution.py:94
  36.2 13.2 %all-gather.15 = bf16[8,1,128]{2,1,0:T(2,128)(2,1)S(1)} all-gather(bf16[1,1,128]{2,1,0:T(2,128)(2,1)S(1)} %convert_bitcast_fusion.17), channel_id=3, replica_groups=mesh['dp'=4,'row'=2,'col'=4] {'row','col'}, dimensions={0}, use_global_device_ids=true | all-gather | bytes 2304 | tf_op jit(solution)/shard_map/all_gather | solution.py:95
  49.5 15.3 %all-gather.17 = bf16[8,1,128]{2,1,0:T(2,128)(2,1)S(1)} all-gather(bf16[1,1,128]{2,1,0:T(2,128)(2,1)S(1)} %convert_bitcast_fusion.15), channel_id=8, replica_groups=mesh['dp'=4,'row'=2,'col'=4] {'row','col'}, dimensions={0}, use_global_device_ids=true | all-gather | bytes 2304 | tf_op jit(solution)/shard_map/all_gather | solution.py:96
  64.8 12.9 %all-gather.18 = bf16[8,1,128]{2,1,0:T(2,128)(2,1)S(1)} all-gather(bf16[1,1,128]{2,1,0:T(2,128)(2,1)S(1)} %convert_bitcast_fusion.14), channel_id=9, replica_groups=mesh['dp'=4,'row'=2,'col'=4] {'row','col'}, dimensions={0}, use_global_device_ids=true | all-gather | bytes 2304 | tf_op jit(solution)/shard_map/all_gather | solution.py:99
  77.7 14.8 %all-gather.19 = bf16[8,1,128]{2,1,0:T(2,128)(2,1)S(1)} all-gather(bf16[1,1,128]{2,1,0:T(2,128)(2,1)S(1)} %convert_bitcast_fusion.13), channel_id=10, replica_groups=mesh['dp'=4,'row'=2,'col'=4] {'row','col'}, dimensions={0}, use_global_device_ids=true | all-gather | bytes 2304 | tf_op jit(solution)/shard_map/all_gather | solution.py:100
  92.5 22.7 %all-gather.20 = bf16[8,1,512]{2,1,0:T(2,128)(2,1)S(1)} all-gather(bf16[1,1,512]{2,1,0:T(2,128)(2,1)S(1)} %reshape.565), channel_id=12, replica_groups=mesh['dp'=4,'row'=2,'col'=4] {'row','col'}, dimensions={0}, use_global_device_ids=true | all-gather | bytes 9216 | tf_op jit(solution)/shard_map/all_gather | solution.py:97
  115.2 12.9 %all-gather.21 = bf16[8,1,128]{2,1,0:T(2,128)(2,1)S(1)} all-gather(bf16[1,1,128]{2,1,0:T(2,128)(2,1)S(1)} %convert_bitcast_fusion.12), channel_id=14, replica_groups=mesh['dp'=4,'row'=2,'col'=4] {'row','col'}, dimensions={0}, use_global_device_ids=true | all-gather | bytes 2304 | tf_op jit(solution)/shard_map/all_gather | solution.py:98
  128.7 14.8 %all-gather.22 = bf16[8,1,128]{2,1,0:T(2,128)(2,1)S(1)} all-gather(bf16[1,1,128]{2,1,0:T(2,128)(2,1)S(1)} %convert_bitcast_fusion.11), channel_id=15, replica_groups=mesh['dp'=4,'row'=2,'col'=4] {'row','col'}, dimensions={0}, use_global_device_ids=true | all-gather | bytes 2304 | tf_op jit(solution)/shard_map/all_gather | solution.py:101
  144.1 13.2 %all-gather.23 = bf16[8,1,128]{2,1,0:T(2,128)(2,1)S(1)} all-gather(bf16[1,1,128]{2,1,0:T(2,128)(2,1)S(1)} %convert_bitcast_fusion.10), channel_id=16, replica_groups=mesh['dp'=4,'row'=2,'col'=4] {'row','col'}, dimensions={0}, use_global_device_ids=true | all-gather | bytes 2304 | tf_op jit(solution)/shard_map/all_gather | solution.py:102
  164.8 4.5 copy.185
  169.3 3.9 bitcast_convert_fusion.1
  174.7 4.5 copy.179
  179.2 3.9 fusion.31
  184.5 26.1 %all-gather.37.cloned.1.call-done = bf16[4096,256]{1,0:T(8,128)(2,1)} async-done(((bf16[512,256]{1,0:T(8,128)(2,1)}), bf16[4096,256]{1,0:T(8,128)(2,1)}) %all-gather.37.cloned.1.call-update) | async-done | bytes 2097168 | tf_op jit(solution)/shard_map/all_gather | solution.py:91
  210.6 4.1 copy.189
  214.8 7.7 fusion.77
  222.4 8.8 fusion
  231.2 8.2 fusion.37
  241.7 95.7 %all-gather.41.cloned.1.call-done = bf16[16384,256]{1,0:T(8,128)(2,1)} async-done(((bf16[2048,256]{1,0:T(8,128)(2,1)}), bf16[16384,256]{1,0:T(8,128)(2,1)}) %all-gather.41.cloned.1.call-update) | async-done | bytes 8388624 | tf_op jit(solution)/shard_map/all_gather | solution.py:93
  337.4 11.6 copy.193
  349.0 7.4 copy.195
  356.4 106.3 %all-gather.39.cloned.1.call-done = bf16[4096,1024]{1,0:T(8,128)(2,1)} async-done(((bf16[512,1024]{1,0:T(8,128)(2,1)}), bf16[4096,1024]{1,0:T(8,128)(2,1)}) %all-gather.39.cloned.1.call-update) | async-done | bytes 8388624 | tf_op jit(solution)/shard_map/all_gather | solution.py:92
  462.6 11.4 copy.191
  474.0 7.6 copy.197
  481.6 25.6 %multiply_convert_fusion.1 = (bf16[512,4096]{1,0:T(8,128)(2,1)S(1)}, f32[512,4096]{1,0:T(8,128)}, f32[512,4096,1]{1,0,2:T(8,128)}) fusion(f32[4096]{0:T(1024)S(1)} %bitcast.410, bf16[4096,512,2]{1,0,2:T(8,128)(2,1)} %bitcast.352, bf16[64,2,8,512]{3,2,1,0:T(8,128)(2,1)S(1)} %bitcast.393), kind=kOutput, calls=%fused_computation.24 | convolution fusion | flops 4433379328 | bytes 30425088 | tf_op jit(solution)/shard_map/trk,rckn->tcn/dot_general | solution.py:28
  507.3 9.4 fusion.79
  522.8 14.8 %fusion.80 = (bf16[4096]{0:T(1024)(128)(2,1)}, bf16[512,4096]{1,0:T(8,128)(2,1)}) fusion(f32[512,4096]{1,0:T(8,128)} %get-tuple-element.61, bf16[4096,4,256]{2,0,1:T(8,128)(2,1)} %bitcast.350, bf16[64,4,8,256]{3,2,1,0:T(8,128)(2,1)S(1)} %bitcast.370, f32[4096]{0:T(1024)S(1)} %bitcast.411, f32[512,4096,1]{1,0,2:T(8,128)} %get-tuple-element.69), kind=kOutput, calls=%fused_computation.166 | convolution fusion | flops 4328517632 | bytes 30433280 | tf_op jit(solution)/shard_map/tcn,rckn->trk/dot_general | solution.py:40
  537.5 8.5 multiply_reduce_fusion.2
  552.4 4.5 copy.219
  559.5 8.9 bitcast_reduce_fusion
  573.1 9.2 fusion.71
  582.3 8.1 multiply_convert_fusion
  596.3 4.2 copy.212
  601.0 6.0 multiply_convert_fusion.2
  610.6 4.2 copy.214
  615.7 9.0 convert_bitcast_fusion
  624.7 11.5 copy.225
  636.3 8.0 reshape.504
  644.4 11.8 convert_bitcast_fusion.1
  656.1 11.6 copy.222
  673.9 39.5 %pmax.7 = f32[16]{0:T(128)S(1)} all-reduce(f32[16]{0:T(128)S(1)} %copy-done.50), channel_id=1, replica_groups=mesh['dp'=4,'row'=2,'col'=4] {'dp','row','col'}, use_global_device_ids=true, to_apply=%region_51.52 | all-reduce | flops 16 | bytes 128 | tf_op jit(solution)/shard_map/pmax | solution.py:211
  713.7 28.5 %all-reduce.9 = (bf16[8,128]{1,0:T(8,128)(2,1)S(1)}, bf16[8,128]{1,0:T(8,128)(2,1)S(1)}, bf16[8,128]{1,0:T(8,128)(2,1)S(1)}, bf16[8,512]{1,0:T(8,128)(2,1)S(1)},...) all-reduce(bf16[8,128]{1,0:T(8,128)(2,1)S(1)} %convert_element_type, ...), channel_id=23, replica_groups=mesh['dp'=4,'row'=2,'col'=4] {'row','col'}, use_global_device_ids=true, to_apply=%region_24.25.clone | all-reduce | flops 12288 | bytes 49152
  745.6 14.3 %all-reduce.10 = (bf16[128]{0:T(256)(128)(2,1)S(1)}, bf16[128]{0:T(256)(128)(2,1)S(1)}, bf16[128]{0:T(256)(128)(2,1)S(1)}, bf16[512]{0:T(512)(128)(2,1)S(1)}, bf...) all-reduce(bf16[128]{0:T(256)(128)(2,1)S(1)} %get-tuple-element.80,, ...), channel_id=1, replica_groups=mesh['dp'=4,'row'=2,'col'=4] {'dp'}, use_global_device_ids=true, to_apply=%region_25.26 | all-reduce | flops 1536 | bytes 6144 | tf_op jit(solution)/shard_map/psum | solution.py:326
  765.0 70.8 %reduce-scatter.9.cloned.1.call-done = bf16[1,512,256]{2,1,0:T(8,128)(2,1)} async-done(((bf16[8,512,256]{2,1,0:T(8,128)(2,1)}), bf16[1,512,256]{2,1,0:T(8,128)(2,1)}) %reduce-scatter.9.cloned.1.call-update) | async-done | bytes 262160 | tf_op jit(solution)/shard_map/reduce_scatter | solution.py:276
  835.9 151.5 %reduce-scatter.17.cloned.1.call-done = bf16[1,2048,256]{2,1,0:T(8,128)(2,1)} async-done(((bf16[8,2048,256]{2,1,0:T(8,128)(2,1)}), bf16[1,2048,256]{2,1,0:T(8,128)(2,1)}) %reduce-scatter.17.cloned.1.call-update) | async-done | bytes 1048592 | tf_op jit(solution)/shard_map/reduce_scatter | solution.py:288
  987.3 150.1 %reduce-scatter.15.cloned.1.call-done = bf16[1,512,1024]{2,1,0:T(8,128)(2,1)} async-done(((bf16[8,512,1024]{2,1,0:T(8,128)(2,1)}), bf16[1,512,1024]{2,1,0:T(8,128)(2,1)}) %reduce-scatter.15.cloned.1.call-update) | async-done | bytes 1048592 | tf_op jit(solution)/shard_map/reduce_scatter | solution.py:285
  1139.7 3.0 fusion.81
  1147.5 59.9 %all-reduce.14.cloned.1.call-done = (bf16[512,256]{1,0:T(8,128)(2,1)}, bf16[512,256]{1,0:T(8,128)(2,1)}, bf16[512,256]{1,0:T(8,128)(2,1)}, bf16[512,256]{1,0:T(8...) async-done(((bf16[512,256]{1,0:T(8,128)(2,1)}, bf16[512,256]{1,0:T(8,128)(2,1)}, bf16[512,256]{1,0:T(8,128)(2,1)}, bf16[512,256]{1,0:T(8,128)(2,1)}, ...) | async-done | bytes 3145744 | tf_op jit(solution)/shard_map/psum | solution.py:320
  (259 shorter events, 85.1 us)
Async XLA Ops:
  7.2 151.0 %all-gather.33.cloned.1.call-start = ((), (), s32[]{:S(2)}) async-start(), calls=%async_computation.13 | async-start | bytes 2359296 | tf_op jit(solution)/shard_map/all_gather | solution.py:88
  9.2 155.6 %all-gather.35.cloned.1.call-start = ((), (), s32[]{:S(2)}) async-start(), calls=%async_computation.14 | async-start | bytes 2359296 | tf_op jit(solution)/shard_map/all_gather | solution.py:89
  11.0 163.6 %all-gather.31.cloned.1.call-start = ((), (), s32[]{:S(2)}) async-start(), calls=%async_computation.12 | async-start | bytes 2359296 | tf_op jit(solution)/shard_map/all_gather | solution.py:90
  12.9 197.7 %all-gather.37.cloned.1.call-start = ((), (), s32[]{:S(2)}) async-start(), calls=%async_computation.15 | async-start | bytes 2359296 | tf_op jit(solution)/shard_map/all_gather | solution.py:91
  14.7 322.7 %all-gather.41.cloned.1.call-start = ((), (), s32[]{:S(2)}) async-start(), calls=%async_computation.17 | async-start | bytes 9437184 | tf_op jit(solution)/shard_map/all_gather | solution.py:93
  15.9 20.4 %copy-start.52 = (f32[128]{0:T(128)S(1)}, f32[128]{0:T(128)}, u32[]{:S(2)}) copy-start(f32[128]{0:T(128)} %param.30) | copy-start | bytes 1540
  15.9 33.6 %copy-start.53 = (f32[128]{0:T(128)S(1)}, f32[128]{0:T(128)}, u32[]{:S(2)}) copy-start(f32[128]{0:T(128)} %param.31) | copy-start | bytes 1540
  15.9 48.9 %copy-start.54 = (f32[128]{0:T(128)S(1)}, f32[128]{0:T(128)}, u32[]{:S(2)}) copy-start(f32[128]{0:T(128)} %param.34) | copy-start | bytes 1540
  15.9 61.8 %copy-start.55 = (f32[128]{0:T(128)S(1)}, f32[128]{0:T(128)}, u32[]{:S(2)}) copy-start(f32[128]{0:T(128)} %param.35) | copy-start | bytes 1540
  15.9 76.6 %copy-start.49 = (f32[512]{0:T(512)S(1)}, f32[512]{0:T(512)}, u32[]{:S(2)}) copy-start(f32[512]{0:T(512)} %param.32) | copy-start | bytes 6148
  15.9 99.3 %copy-start.56 = (f32[128]{0:T(128)S(1)}, f32[128]{0:T(128)}, u32[]{:S(2)}) copy-start(f32[128]{0:T(128)} %param.33) | copy-start | bytes 1540
  15.9 112.8 %copy-start.57 = (f32[128]{0:T(128)S(1)}, f32[128]{0:T(128)}, u32[]{:S(2)}) copy-start(f32[128]{0:T(128)} %param.36) | copy-start | bytes 1540
  15.9 128.2 %copy-start.58 = (f32[128]{0:T(128)S(1)}, f32[128]{0:T(128)}, u32[]{:S(2)}) copy-start(f32[128]{0:T(128)} %param.37) | copy-start | bytes 1540
  15.9 142.0 %copy-start.41 = (s32[512]{0:T(512)S(1)}, s32[512]{0:T(512)}, u32[]{:S(2)}) copy-start(s32[512]{0:T(512)} %param.21) | copy-start | bytes 6148
  16.0 446.6 %all-gather.39.cloned.1.call-start = ((), (), s32[]{:S(2)}) async-start(), calls=%async_computation.16 | async-start | bytes 9437184 | tf_op jit(solution)/shard_map/all_gather | solution.py:92
  18.9 745.8 %reduce-scatter.13.cloned.1.call-start = ((), (), s32[]{:S(2)}) async-start(), calls=%async_computation.9 | async-start | bytes 2359296 | tf_op jit(solution)/shard_map/reduce_scatter | solution.py:282
  19.1 160.0 %copy-start.23 = (bf16[512,1024]{1,0:T(8,128)(2,1)}, bf16[512,1024]{1,0:T(8,128)(2,1)S(1)}, u32[]{:S(2)}) copy-start(bf16[512,1024]{1,0:T(8,128)(2,1)S(1)} %convert_element_type.490) | copy-start | bytes 3145732
  164.8 50.0 %copy-start.5 = (bf16[512,1024]{0,1:T(8,128)(2,1)}, bf16[512,1024]{0,1:T(8,128)(2,1)S(1)}, u32[]{:S(2)}) copy-start(bf16[512,1024]{0,1:T(8,128)(2,1)S(1)} %copy.184) | copy-start | bytes 3145732
  174.6 40.1 %copy-start.3 = (bf16[512,1024]{0,1:T(8,128)(2,1)}, bf16[512,1024]{0,1:T(8,128)(2,1)S(1)}, u32[]{:S(2)}) copy-start(bf16[512,1024]{0,1:T(8,128)(2,1)S(1)} %copy.187) | copy-start | bytes 3145732
  184.5 46.7 %copy-start.13 = (bf16[512,1024]{0,1:T(8,128)(2,1)}, bf16[512,1024]{0,1:T(8,128)(2,1)S(1)}, u32[]{:S(2)}) copy-start(bf16[512,1024]{0,1:T(8,128)(2,1)S(1)} %copy.181) | copy-start | bytes 3145732
  222.4 8.8 copy-start.31
  231.2 8.3 copy-start.37
  231.2 8.3 copy-start.20
  231.2 8.3 copy-start.22
  241.7 239.9 %copy-start.28 = (bf16[512,1024]{1,0:T(8,128)(2,1)}, bf16[512,1024]{1,0:T(8,128)(2,1)S(1)}, u32[]{:S(2)}) copy-start(bf16[512,1024]{1,0:T(8,128)(2,1)S(1)} %fusion.32) | copy-start | bytes 3145732
  481.6 25.6 %copy-start.46 = (f32[8,1,128]{2,1,0:T(1,128)S(1)}, f32[8,1,128]{2,1,0:T(1,128)}, u32[]{:S(2)}) copy-start(f32[8,1,128]{2,1,0:T(1,128)} %convert_element_type.645) | copy-start | bytes 12292
  507.2 9.4 copy-start.59
  507.2 9.8 copy-start.11
  507.3 9.8 copy-start.39
  518.4 19.1 %slice-start = ((s8[8388608]{0:T(1024)(128)(4,1)}), s8[4194304]{0:T(1024)(128)(4,1)S(1)}, s32[]{:S(2)}) async-start(s8[8388608]{0:T(1024)(128)(4,1)} %bitcast.347), calls=%async_computation.19 | async-start | bytes 8388608
  522.7 14.8 %copy-start.14 = (bf16[512,1024]{1,0:T(8,128)(2,1)}, bf16[512,1024]{1,0:T(8,128)(2,1)S(1)}, u32[]{:S(2)}) copy-start(bf16[512,1024]{1,0:T(8,128)(2,1)S(1)} %get-tuple-element.53) | copy-start | bytes 3145732
  522.7 14.8 %slice-start.1 = ((s8[8388608]{0:T(1024)(128)(4,1)}), s8[4194304]{0:T(1024)(128)(4,1)S(1)}, s32[]{:S(2)}) async-start(s8[8388608]{0:T(1024)(128)(4,1)} %bitcast.347), calls=%async_computation.20 | async-start | bytes 8388608
  556.9 207.8 %reduce-scatter.11.cloned.1.call-start = ((), (), s32[]{:S(2)}) async-start(), calls=%async_computation.8 | async-start | bytes 2359296 | tf_op jit(solution)/shard_map/reduce_scatter | solution.py:279
  559.5 9.9 copy-start.24
  573.1 192.0 %reduce-scatter.7.cloned.1.call-start = ((), (), s32[]{:S(2)}) async-start(), calls=%async_computation.6 | async-start | bytes 2359296 | tf_op jit(solution)/shard_map/reduce_scatter | solution.py:273
  582.3 8.1 copy-start.4
  600.5 235.3 %reduce-scatter.9.cloned.1.call-start = ((), (), s32[]{:S(2)}) async-start(), calls=%async_computation.7 | async-start | bytes 2359296 | tf_op jit(solution)/shard_map/reduce_scatter | solution.py:276
  614.9 372.5 %reduce-scatter.17.cloned.1.call-start = ((), (), s32[]{:S(2)}) async-start(), calls=%async_computation.11 | async-start | bytes 9437184 | tf_op jit(solution)/shard_map/reduce_scatter | solution.py:288
  636.3 8.1 copy-start.29
  636.3 501.1 %reduce-scatter.15.cloned.1.call-start = ((), (), s32[]{:S(2)}) async-start(), calls=%async_computation.10 | async-start | bytes 9437184 | tf_op jit(solution)/shard_map/reduce_scatter | solution.py:285
  667.8 539.6 %all-reduce.14.cloned.1.call-start = ((), (), s32[]{:S(2)}) async-start(), calls=%async_computation.18 | async-start | bytes 6291456 | tf_op jit(solution)/shard_map/psum | solution.py:320
  672.3 41.4 %copy-start.45 = (bf16[4096]{0:T(1024)(128)(2,1)S(1)}, bf16[4096]{0:T(1024)(128)(2,1)}, u32[]{:S(2)}) copy-start(bf16[4096]{0:T(1024)(128)(2,1)} %get-tuple-element.78) | copy-start | bytes 24580
  672.3 41.4 %copy-start.42 = (bf16[1024]{0:T(1024)(128)(2,1)S(1)}, bf16[1024]{0:T(1024)(128)(2,1)}, u32[]{:S(2)}) copy-start(bf16[1024]{0:T(1024)(128)(2,1)} %get-tuple-element.26) | copy-start | bytes 6148
  672.3 41.4 %copy-start.43 = (bf16[1024]{0:T(1024)(128)(2,1)S(1)}, bf16[1024]{0:T(1024)(128)(2,1)}, u32[]{:S(2)}) copy-start(bf16[1024]{0:T(1024)(128)(2,1)} %get-tuple-element.52) | copy-start | bytes 6148
  672.3 41.4 %copy-start.44 = (bf16[1024]{0:T(1024)(128)(2,1)S(1)}, bf16[1024]{0:T(1024)(128)(2,1)}, u32[]{:S(2)}) copy-start(bf16[1024]{0:T(1024)(128)(2,1)} %get-tuple-element.54) | copy-start | bytes 6148
  672.3 41.4 %copy-start.47 = (bf16[1024]{0:T(1024)(128)(2,1)S(1)}, bf16[1024]{0:T(1024)(128)(2,1)}, u32[]{:S(2)}) copy-start(bf16[1024]{0:T(1024)(128)(2,1)} %get-tuple-element.24) | copy-start | bytes 6148
  672.3 41.4 %copy-start.48 = (bf16[1024]{0:T(1024)(128)(2,1)S(1)}, bf16[1024]{0:T(1024)(128)(2,1)}, u32[]{:S(2)}) copy-start(bf16[1024]{0:T(1024)(128)(2,1)} %get-tuple-element.27) | copy-start | bytes 6148
  713.5 429.3 %copy-start.63 = (f32[16]{0:T(128)}, f32[16]{0:T(128)S(1)}, u32[]{:S(2)}) copy-start(f32[16]{0:T(128)S(1)} %pmax.7) | copy-start | bytes 196
  (31 other events, 96.7 us)
Sparse Core Ops, SparseCore 0:
  10.7 48.4 all-gather.32
  61.9 47.6 all-gather.34
  112.3 47.7 all-gather.30
  162.6 47.9 all-gather.36
  213.2 124.1 all-gather.40
  339.9 122.6 all-gather.38
  557.0 65.6 reduce-scatter.12
  626.3 67.3 reduce-scatter.10
  697.2 67.7 reduce-scatter.6
  768.4 67.3 reduce-scatter.8
  839.5 147.7 reduce-scatter.16
  990.8 146.5 reduce-scatter.14
  1140.2 67.1 all-reduce.13
where the time goes:
time: 1240 us; the launch traced here: 1220 us
  waiting for transfers between devices  661 us (53%)
  blocking collectives  219 us (18%)
  matrix products  149 us (12%)
  local copies, waits for them, and re-layouts  123 us (10%)
  other arithmetic  53.2 us (4%)
  between operations  16.5 us (1%)
    reduce_scatter x1, waiting for transfers between devices, on_device(): lax.psum_scatter(terms[5].astype(jnp.bfloat16), ('row', 'col'), scatter_d...  151 us
    reduce_scatter x1, waiting for transfers between devices, on_device(): lax.psum_scatter(terms[4].astype(jnp.bfloat16), ('row', 'col'), scatter_d...  150 us
    all_gather x1, waiting for transfers between devices, fetch_params(): lax.all_gather(wire_items[4], ('row', 'col'), axis=0, tiled=True)  106 us
    all_gather x1, waiting for transfers between devices, fetch_params(): lax.all_gather(wire_items[5], ('row', 'col'), axis=0, tiled=True)  95.7 us
    reduce_scatter x1, waiting for transfers between devices, on_device(): lax.psum_scatter(terms[1].astype(jnp.bfloat16), ('row', 'col'), scatter_d...  70.8 us
    psum x1, waiting for transfers between devices, on_device(): lax.psum(parted[0][0].astype(jnp.bfloat16), 'dp').astype(jnp.float32)  59.9 us
    reshape x12, local copies, waits for them, and re-layouts, unpack(): shard_item.reshape(row_count, col_count, shard_item.shape[1], shard_item....  57.1 us
    dot_general x6, matrix products, apply_weight(): jnp.einsum('trk,rckn->tcn', operand.reshape(token_count, row_count, rows_...  46.4 us
  transfers between devices with their start and end apart: 13, of which 8 were waited for; matrix products, arithmetic and copies ran while one was open for 18% of the time, Pallas kernels for 0%

commit v1 on v0

v1 whole, which is shorter than its diff:
```python
import functools
import jax
import jax.numpy as jnp
from jax import lax
from jax.experimental import pallas as pl
from jax.experimental.pallas import tpu as pltpu
from jax.sharding import PartitionSpec as P

MESH = pl.DeviceIdType.MESH

LAGS = (0, 2, 5, 60)
SEQ, H, DH = 512, 16, 64

def place():
    dp = lax.axis_index("dp")
    return lax.axis_index("row"), lax.axis_index("col"), dp, dp % 2, (dp // 2) % 2


def core_peer(dp):
    return {"dp": dp + 1 - 2 * (dp % 2)}


def y_peer(dp):
    side = (dp // 2) % 2
    return {"dp": dp + 2 - 4 * side}


class Sends:
    def __init__(self):
        self.items = []

    def start(self, when, src, dst, send_sem, recv_sem, device):
        copy = pltpu.make_async_remote_copy(
            src_ref=src, dst_ref=dst, send_sem=send_sem, recv_sem=recv_sem,
            device_id=device, device_id_type=MESH,
        )
        self.items.append((when, copy))
        if when is None:
            copy.start()
        else:
            pl.when(when)(copy.start)

    def finish(self):
        for when, copy in self.items:
            if when is None:
                copy.wait_send()
            else:
                pl.when(when)(copy.wait_send)


def wait_arrival(dst, recv_sem, device):
    pltpu.make_async_remote_copy(
        src_ref=dst, dst_ref=dst, send_sem=recv_sem, recv_sem=recv_sem,
        device_id=device, device_id_type=MESH,
    ).wait_recv()


def group_barrier(rows, cols):
    row, col, dp, _, _ = place()
    barrier = pltpu.get_barrier_semaphore()
    peers = [core_peer(dp), y_peer(dp)]
    mine = row * cols + col
    for step in range(1, rows * cols):
        other = (mine + step) % (rows * cols)
        peers.append({"row": other // cols, "col": other % cols})
    for peer in peers:
        pl.semaphore_signal(barrier, inc=1, device_id=peer, device_id_type=MESH)
    pl.semaphore_wait(barrier, len(peers))


def entries_of(heights):
    found = []
    for m, height in enumerate(heights):
        found.append((m, True, 0, height * 3 // 16))
        found.append((m, False, height * 3 // 4, height // 8))
    return found


def gather_kernel(rows, cols, entries, ahead, *refs):
    count = 1 + max(entry[0] for entry in entries)
    number = len(entries)
    blocks, vec = refs[:count], refs[count]
    wholes, vecs = refs[count + 1 : 2 * count + 1], refs[2 * count + 1]
    (z_in, x_in, y_in, c_in, v_in, z_out, x_out, y_out, c_out, v_out, own_sem, own_vec) = refs[2 * count + 2 :]
    row, col, dp, core, side = place()
    group_barrier(rows, cols)
    sends = Sends()
    other = 1 - row
    x_dev, y_dev, c_dev = {"row": other}, y_peer(dp), core_peer(dp)
    mine = row * cols + col

    for step in range(1, rows * cols):
        peer = (mine + step) % (rows * cols)
        sends.start(None, vec, vecs.at[mine], v_out.at[step], v_in.at[mine],
                    {"row": peer // cols, "col": peer % cols})

    def offset(e, of_core, of_side):
        _, paired, base, part = entries[e]
        return base + ((of_core * 2 + of_side) * part if paired else of_core * part)

    def region(e, of_row, of_col, of_core, of_side):
        m, _, _, part = entries[e]
        height, width = blocks[m].shape
        start = of_row * height + offset(e, of_core, of_side)
        return wholes[m].at[pl.ds(pl.multiple_of(start, 16), part),
                            pl.ds(pl.multiple_of(of_col * width, width), width)]

    def own_part(e):
        m, _, _, part = entries[e]
        return blocks[m].at[pl.ds(pl.multiple_of(offset(e, core, side), 16), part), :]

    def send_own(e):
        dst = region(e, row, col, core, side)
        src = own_part(e)
        for step in range(1, cols):
            sends.start(col + step < cols, src, dst, z_out.at[e, step, 0], z_in.at[e, col], {"col": jnp.minimum(col + step, cols - 1)})
            sends.start(col >= step, src, dst, z_out.at[e, step, 1], z_in.at[e, col], {"col": jnp.maximum(col - step, 0)})
            if step == 1:
                sends.start(None, src, dst, x_out.at[e, col], x_in.at[e, col], x_dev)

    def keep_own(m):
        height, width = blocks[m].shape
        return pltpu.make_async_copy(
            blocks[m],
            wholes[m].at[pl.ds(pl.multiple_of(row * height, height), height),
                         pl.ds(pl.multiple_of(col * width, width), width)],
            own_sem.at[m])

    def share(m, of_row, of_col, when):
        piece = region(m, of_row, of_col, core, side)
        if entries[m][1]:
            sends.start(when, piece, piece, y_out.at[m, of_row, of_col], y_in.at[m, of_row, of_col], y_dev)
        sends.start(when, piece, piece, c_out.at[m, of_row, of_col, 0], c_in.at[m, of_row, of_col, 0], c_dev)

    def columns(step):
        if step == 0:
            return [(0, None, col)]
        return [(-1, col >= step, jnp.maximum(col - step, 0)),
                (1, col + step < cols, jnp.minimum(col + step, cols - 1))]

    def guarded(when, body):
        if when is None:
            body()
        else:
            pl.when(when)(body)

    def both(a, b):
        return b if a is None else jnp.logical_and(a, b)

    def z_stage(m, step):
        if step == 0:
            if m + ahead < number:
                send_own(m + ahead)
            return
        for sign, when, at in columns(step):
            piece = region(m, row, at, core, side)
            guarded(when, lambda: wait_arrival(piece, z_in.at[m, at], {"col": col}))
            sends.start(when, piece, piece, x_out.at[m, at], x_in.at[m, at], x_dev)
            share(m, row, at, when)

    def x_stage(m, step):
        for _, when, at in columns(step):
            piece = region(m, other, at, core, side)
            guarded(when, lambda: wait_arrival(piece, x_in.at[m, at], x_dev))
            share(m, other, at, when)

    def y_stage(m, step):
        if not entries[m][1]:
            return
        for _, when, at in columns(step):
            for of_row in (row, other):
                if step == 0 and of_row is row:
                    continue
                piece = region(m, of_row, at, core, 1 - side)
                guarded(when, lambda: wait_arrival(piece, y_in.at[m, of_row, at], y_dev))
                sends.start(when, piece, piece, c_out.at[m, of_row, at, 1], c_in.at[m, of_row, at, 1], c_dev)

    def c_stage(m, step):
        for _, when, at in columns(step):
            for of_row in (row, other):
                if step == 0 and of_row is row:
                    continue
                piece = region(m, of_row, at, 1 - core, side)
                guarded(when, lambda: wait_arrival(piece, c_in.at[m, of_row, at, 0], c_dev))
                if entries[m][1]:
                    far = region(m, of_row, at, 1 - core, 1 - side)
                    guarded(when, lambda: wait_arrival(far, c_in.at[m, of_row, at, 1], c_dev))

    for e in range(ahead):
        send_own(e)
    for m in range(count):
        keep_own(m).start()
    keep_vec = pltpu.make_async_copy(vec, vecs.at[mine], own_vec)
    keep_vec.start()
    items = [(e, step) for e in range(number) for step in range(cols)]
    for tick in range(len(items) + LAGS[-1]):
        for lag, stage in zip(LAGS, (z_stage, x_stage, y_stage, c_stage)):
            if 0 <= tick - lag < len(items):
                stage(*items[tick - lag])
    for step in range(1, rows * cols):
        peer = (mine + step) % (rows * cols)
        wait_arrival(vecs.at[peer], v_in.at[peer], {"row": peer // cols, "col": peer % cols})
    for m in range(count):
        keep_own(m).wait()
    keep_vec.wait()
    sends.finish()


def gather_all(blocks, vec, ahead=3):
    rows, cols = lax.axis_size("row"), lax.axis_size("col")
    count = len(blocks)
    wholes = [jax.ShapeDtypeStruct((b.shape[0] * rows, b.shape[1] * cols), b.dtype) for b in blocks]
    out_shape = (*wholes, jax.ShapeDtypeStruct((rows * cols, *vec.shape), vec.dtype))
    entries = entries_of([b.shape[0] for b in blocks])
    number = len(entries)
    dma = pltpu.SemaphoreType.DMA
    return pl.pallas_call(
        functools.partial(gather_kernel, rows, cols, entries, ahead),
        out_shape=out_shape,
        in_specs=[pl.BlockSpec(memory_space=pltpu.VMEM)] * (count + 1),
        out_specs=[pl.BlockSpec(memory_space=pl.ANY)] * (count + 1),
        scratch_shapes=[
            dma((number, cols)), dma((number, cols)), dma((number, rows, cols)), dma((number, rows, cols, 2)), dma((rows * cols,)),
            dma((number, cols, 2)), dma((number, cols)), dma((number, rows, cols)), dma((number, rows, cols, 2)), dma((rows * cols,)),
            dma((count,)), dma,
        ],
        compiler_params=pltpu.CompilerParams(collective_id=0, has_side_effects=True),
        name="gather_all",
    )(*blocks, vec)


RL = (0, 1, 2, 3, 4, 5, 6)

def reduce_entries(heights):
    found = []
    for m, height in enumerate(heights):
        found.append((m, True, 0, height // 8))
        found.append((m, False, height // 2, height // 4))
    return found


def add_into(into, other):
    height, width = into.shape
    rows = max(16, min(height, 65536 // width // 16 * 16))
    while height % rows:
        rows -= 16

    @pl.loop(0, height // rows)
    def _(i):
        at = pl.ds(pl.multiple_of(i * rows, rows), rows)
        into[at, :] = into[at, :] + other[at, :]


def reduce_kernel(rows, cols, entries, *refs):
    count = 1 + max(entry[0] for entry in entries)
    number = len(entries)
    terms, vec = refs[:count], refs[count]
    outs, vec_out = refs[count + 1 : 2 * count + 1], refs[2 * count + 1]
    rest = list(refs[2 * count + 2 :])
    take = lambda n: [rest.pop(0) for _ in range(n)]
    acc, c_land, y_land, x_land, z_land, f_land = (take(number) for _ in range(6))
    full = take(count)
    v_acc, v_pair, v_cols = take(3)
    (load_sem, c_in, y_in, x_in, z_in, f_in, g_in, vp_in, vc_in,
     c_out, y_out, x_out, z_out, f_out, g_out, vp_out, vc_out) = rest
    row, col, dp, core, side = place()
    group_barrier(rows, cols)
    sends = Sends()
    other = 1 - row
    x_dev, y_dev, c_dev = {"row": other}, y_peer(dp), core_peer(dp)

    def band(e, of_row, of_core):
        m, paired, base, part = entries[e]
        height = terms[m].shape[0] // rows
        size = 2 * part if paired else part
        start = of_row * height + base + of_core * size
        return terms[m].at[pl.ds(pl.multiple_of(start, 16), size), :]

    def load(e):
        return [pltpu.make_async_copy(band(e, r, core), acc[e].at[r], load_sem.at[e, r]) for r in range(rows)]

    for e in range(number):
        for r in range(rows):
            sends.start(None, band(e, r, 1 - core), c_land[e].at[r], c_out.at[e, r], c_in.at[e, r], c_dev)
        for copy in load(e):
            copy.start()

    def mine(e, r, of_side):
        _, paired, _, part = entries[e]
        if paired:
            return acc[e].at[r, pl.ds(pl.multiple_of(of_side * part, 16), part), :]
        return acc[e].at[r]

    def columns(ref, e, at):
        width = terms[entries[e][0]].shape[1] // cols
        return ref.at[:, pl.ds(pl.multiple_of(at * width, width), width)]

    def send_x(e):
        sends.start(None, mine(e, other, side), x_land[e], x_out.at[e], x_in.at[e], x_dev)

    def core_stage(e):
        for copy in load(e):
            copy.wait()
        for r in range(rows):
            wait_arrival(c_land[e].at[r], c_in.at[e, r], c_dev)
        if entries[e][1]:
            for r in range(rows):
                add_into(mine(e, r, 1 - side), y_view(e, r))
                sends.start(None, mine(e, r, 1 - side), y_land[e].at[r], y_out.at[e, r], y_in.at[e, r], y_dev)
            for r in range(rows):
                add_into(mine(e, r, side), y_view(e, r, side))
        else:
            add_into(acc[e].at[other], c_land[e].at[other])
            send_x(e)
            add_into(acc[e].at[row], c_land[e].at[row])

    def y_view(e, r, of_side=None):
        part = entries[e][3]
        at = 1 - side if of_side is None else of_side
        return c_land[e].at[r, pl.ds(pl.multiple_of(at * part, 16), part), :]

    def y_stage(e):
        if not entries[e][1]:
            return
        for r in (other, row):
            wait_arrival(y_land[e].at[r], y_in.at[e, r], y_dev)
            add_into(mine(e, r, side), y_land[e].at[r])
            if r is other:
                send_x(e)

    def x_stage(e):
        wait_arrival(x_land[e], x_in.at[e], x_dev)
        add_into(mine(e, row, side), x_land[e])
        for step in range(1, cols):
            for way, ok, to in ((0, col + step < cols, jnp.minimum(col + step, cols - 1)),
                                (1, col >= step, jnp.maximum(col - step, 0))):
                sends.start(ok, columns(mine(e, row, side), e, to), z_land[e].at[col],
                            z_out.at[e, step, way], z_in.at[e, col], {"col": to})

    def out_rows(e, of_core, of_side):
        m, paired, base, part = entries[e]
        start = base + ((of_core * 2 + of_side) * part if paired else of_core * part)
        return full[m].at[pl.ds(pl.multiple_of(start, 16), part), :]

    def z_stage(e):
        total = columns(mine(e, row, side), e, col)
        for step in range(1, cols):
            for ok, at in ((col + step < cols, jnp.minimum(col + step, cols - 1)),
                           (col >= step, jnp.maximum(col - step, 0))):
                @pl.when(ok)
                def _():
                    wait_arrival(z_land[e].at[at], z_in.at[e, at], {"col": at})
                    add_into(total, z_land[e].at[at])
        if entries[e][1]:
            sends.start(None, total, out_rows(e, core, side), f_out.at[e], f_in.at[e], y_dev)
            sends.start(None, total, out_rows(e, core, side), g_out.at[e, 0], g_in.at[e, 0], c_dev)
            out_rows(e, core, side)[...] = total[...]
        else:
            sends.start(None, total, f_land[e], f_out.at[e], f_in.at[e], y_dev)

    def final_stage(e):
        m = entries[e][0]
        if entries[e][1]:
            piece = out_rows(e, core, 1 - side)
            wait_arrival(piece, f_in.at[e], y_dev)
            sends.start(None, piece, piece, g_out.at[e, 1], g_in.at[e, 1], c_dev)
        else:
            total = columns(mine(e, row, side), e, col)
            wait_arrival(f_land[e], f_in.at[e], y_dev)
            piece = out_rows(e, core, side)
            piece[...] = total[...] + f_land[e][...]
            sends.start(None, piece, piece, g_out.at[e, 0], g_in.at[e, 0], c_dev)

    def out_stage(e):
        m = entries[e][0]
        wait_arrival(out_rows(e, 1 - core, side), g_in.at[e, 0], c_dev)
        if entries[e][1]:
            wait_arrival(out_rows(e, 1 - core, 1 - side), g_in.at[e, 1], c_dev)
        _, paired, base, part = entries[e]
        size = 4 * part if paired else 2 * part

        @pl.loop(0, size // 32)
        def _(i):
            at = pl.ds(pl.multiple_of(base + i * 32, 32), 32)
            outs[m][at, :] = full[m][at, :].astype(jnp.float32)

    v_rows = v_acc.shape[0]
    merge = lambda a, b: jnp.concatenate([a[: v_rows - 8] + b[: v_rows - 8], jnp.maximum(a[v_rows - 8 :], b[v_rows - 8 :])])
    v_devs = (c_dev, y_dev, x_dev)

    def vec_send(k):
        src = vec if k == 0 else v_acc.at[k - 1]
        sends.start(None, src, v_pair.at[k], vp_out.at[k], vp_in.at[k], v_devs[k])

    def vec_merge(k):
        wait_arrival(v_pair.at[k], vp_in.at[k], v_devs[k])
        before = vec[...] if k == 0 else v_acc_load(k - 1)
        v_acc.at[k][...] = merge(before, v_pair[k])

    def v_acc_load(k):
        return v_acc[k]

    def vec_cols():
        for step in range(1, cols):
            to = (col + step) % cols
            sends.start(None, v_acc.at[2], v_cols.at[col], vc_out.at[step], vc_in.at[col], {"col": to})
        v_cols[pl.ds(col, 1)] = v_acc[2][None]

    def vec_last():
        for step in range(1, cols):
            at = (col + step) % cols
            wait_arrival(v_cols.at[at], vc_in.at[at], {"col": at})
        total = v_cols[0]
        for k in range(1, cols):
            total = merge(total, v_cols[k])
        vec_out[...] = total

    v_rows = v_acc.shape[1]
    steps = [lambda: vec_send(0), lambda: (vec_merge(0), vec_send(1)), lambda: (vec_merge(1), vec_send(2)),
             lambda: (vec_merge(2), vec_cols()), vec_last]
    stages = (core_stage, y_stage, x_stage, z_stage, final_stage, out_stage)
    for tick in range(number + RL[5]):
        for lag, stage in zip(RL, stages):
            if 0 <= tick - lag < number:
                stage(tick - lag)
        if tick < len(steps):
            steps[tick]()
    sends.finish()


def reduce_all(terms, vec, order):
    rows, cols = lax.axis_size("row"), lax.axis_size("col")
    count = len(terms)
    heights = [t.shape[0] // rows for t in terms]
    widths = [t.shape[1] for t in terms]
    pairs = reduce_entries(heights)
    entries = [entry for m in order for entry in pairs if entry[0] == m]
    number = len(entries)
    low = jnp.bfloat16
    sizes = [(2 * part if paired else part, part, widths[m]) for m, paired, _, part in entries]
    vm = pltpu.VMEM
    dma = pltpu.SemaphoreType.DMA
    scratch = (
        [vm((rows, band, width), low) for band, _, width in sizes]
        + [vm((rows, band, width), low) for band, _, width in sizes]
        + [vm((rows, part, width) if entries[e][1] else (rows, 16, 128), low) for e, (_, part, width) in enumerate(sizes)]
        + [vm((part, width), low) for _, part, width in sizes]
        + [vm((cols, part, width // cols), low) for _, part, width in sizes]
        + [vm((part, width // cols), low) for _, part, width in sizes]
        + [vm((heights[m], widths[m] // cols), low) for m in range(count)]
        + [vm((3, *vec.shape), jnp.float32), vm((3, *vec.shape), jnp.float32), vm((cols, *vec.shape), jnp.float32)]
        + [dma((number, rows)), dma((number, rows)), dma((number, rows)), dma((number,)), dma((number, cols)),
           dma((number,)), dma((number, 2)), dma((3,)), dma((cols,)),
           dma((number, rows)), dma((number, rows)), dma((number,)), dma((number, cols, 2)),
           dma((number,)), dma((number, 2)), dma((3,)), dma((cols,))]
    )
    out_shape = tuple(jax.ShapeDtypeStruct((heights[m], widths[m] // cols), jnp.float32) for m in range(count))
    return pl.pallas_call(
        functools.partial(reduce_kernel, rows, cols, entries),
        out_shape=(*out_shape, jax.ShapeDtypeStruct(vec.shape, jnp.float32)),
        in_specs=[pl.BlockSpec(memory_space=pl.ANY)] * count + [pl.BlockSpec(memory_space=pltpu.VMEM)],
        out_specs=[pl.BlockSpec(memory_space=pltpu.VMEM)] * (count + 1),
        scratch_shapes=scratch,
        compiler_params=pltpu.CompilerParams(collective_id=1, has_side_effects=True, vmem_limit_bytes=64000 * 1024),
        name="reduce_all",
    )(*terms, vec)


norm_eps = 1e-12
neg_fill = -1e30
low_type = jnp.bfloat16


def norm_rows(values, gain_vec, shift_vec):
    center = values - jnp.mean(values, axis=-1, keepdims=True)
    spread = jnp.mean(center * center, axis=-1, keepdims=True)
    return center * lax.rsqrt(spread + norm_eps) * gain_vec + shift_vec


def gelu_exact(values):
    return jax.nn.gelu(values, approximate=False)


def forward_dot(operand, weight):
    return jnp.dot(operand, weight, preferred_element_type=jnp.float32)


def back_dot(gradient, weight):
    return lax.dot_general(gradient, weight, (((1,), (1,)), ((), ())), preferred_element_type=jnp.float32)


def weight_term(operand, gradient):
    return lax.dot_general(operand, gradient, (((0,), (0,)), ((), ())),
                           preferred_element_type=jnp.float32).astype(low_type)


def column_sum(gradient_low):
    return jnp.sum(gradient_low, axis=0, dtype=jnp.float32)


def masked_scores(query_heads, key_heads, allowed):
    scores = jnp.einsum(
        "sqhd,skhd->shqk", query_heads, key_heads, preferred_element_type=jnp.float32
    ) * DH ** (-0.5)
    return jnp.where(allowed, scores, neg_fill)


def vector_rows(vectors):
    return jnp.concatenate([v.reshape(-1, 128) for v in vectors])


def on_device(tokens, segment_ids, cotangent, weight_query, weight_key, weight_value, weight_output, weight_inner,
              weight_outer, bias_query, bias_value, bias_output, bias_inner, bias_outer, gain_attn, shift_attn,
              gain_block, shift_block, tau_num, tau_den):
    rows, cols = lax.axis_size("row"), lax.axis_size("col")
    groups = rows * cols
    matrices = (weight_query, weight_key, weight_value, weight_output, weight_inner, weight_outer)
    vectors = (bias_query, bias_value, bias_output, bias_inner, bias_outer, gain_attn, shift_attn, gain_block, shift_block)
    lengths = [v.shape[0] for v in vectors]
    spread = [n * groups for n in lengths]
    flat = jnp.concatenate(vectors).astype(low_type)
    vec_rows = -(-flat.shape[0] // 2048) * 16
    flat = jnp.pad(flat, (0, vec_rows * 128 - flat.shape[0])).reshape(vec_rows, 128)
    gathered = gather_all([m.astype(low_type) for m in matrices], flat)
    whole_query, whole_key, whole_value, whole_output, whole_inner, whole_outer = gathered[:6]
    all_vecs = gathered[6].reshape(groups, -1)
    full, start = [], 0
    for n in lengths:
        full.append(all_vecs[:, start : start + n].reshape(-1).astype(jnp.float32))
        start += n
    (add_query, add_value, add_output, add_inner, add_outer,
     scale_attn, offset_attn, scale_block, offset_block) = full

    token_count = tokens.shape[0]
    seq_count = token_count // SEQ
    head_shape = (seq_count, SEQ, H, DH)
    token_low = tokens.astype(low_type)
    query_low = (forward_dot(token_low, whole_query) + add_query).astype(low_type)
    key_low = forward_dot(token_low, whole_key).astype(low_type)
    value_low = (forward_dot(token_low, whole_value) + add_value).astype(low_type)
    query_heads = query_low.reshape(head_shape)
    key_heads = key_low.reshape(head_shape)
    value_heads = value_low.reshape(head_shape)
    segment_rows = segment_ids.reshape(seq_count, SEQ)
    allowed = (segment_rows[:, :, None] == segment_rows[:, None, :])[:, None, :, :]
    masked = masked_scores(query_heads, key_heads, allowed)
    local_top = jnp.max(masked, axis=(0, 2, 3))
    row_top = jnp.max(masked, axis=-1, keepdims=True)
    raised = jnp.exp(masked - row_top)
    row_total = jnp.sum(raised, axis=-1, keepdims=True)
    attend = raised / row_total
    log_total = row_top + jnp.log(row_total)
    context = jnp.einsum("shqk,skhd->sqhd", attend.astype(low_type), value_heads, preferred_element_type=jnp.float32)
    context_low = context.reshape(token_count, H * DH).astype(low_type)
    first_sum = tokens + forward_dot(context_low, whole_output) + add_output
    normed = norm_rows(first_sum, scale_attn, offset_attn)
    normed_low = normed.astype(low_type)
    hidden_pre = forward_dot(normed_low, whole_inner) + add_inner
    activated_low = gelu_exact(hidden_pre).astype(low_type)
    second_sum = normed + forward_dot(activated_low, whole_outer) + add_outer
    output = norm_rows(second_sum, scale_block, offset_block)
    grad_second, grad_scale_block, grad_offset_block = jax.vjp(norm_rows, second_sum, scale_block, offset_block)[1](cotangent)
    outer_grad_low = grad_second.astype(low_type)
    act_grad = back_dot(outer_grad_low, whole_outer)
    hidden_grad_low = jax.vjp(gelu_exact, hidden_pre)[1](act_grad)[0].astype(low_type)
    normed_grad = grad_second + back_dot(hidden_grad_low, whole_inner)
    grad_first, grad_scale_attn, grad_offset_attn = jax.vjp(norm_rows, first_sum, scale_attn, offset_attn)[1](normed_grad)
    branch_grad_low = grad_first.astype(low_type)
    context_grad_low = back_dot(branch_grad_low, whole_output).astype(low_type)
    masked_again = masked_scores(query_heads, key_heads, allowed)
    attend_again = jnp.exp(masked_again - log_total)
    attend_low = attend_again.astype(low_type)
    context_grad_heads = context_grad_low.reshape(head_shape)
    value_grad = jnp.einsum("shqk,sqhd->skhd", attend_low, context_grad_heads, preferred_element_type=jnp.float32)
    attend_grad = jnp.einsum("sqhd,skhd->shqk", context_grad_heads, value_heads, preferred_element_type=jnp.float32)
    score_grad = attend_again * (attend_grad - jnp.sum(attend_again * attend_grad, axis=-1, keepdims=True))
    score_grad_low = score_grad.astype(low_type)
    query_grad = jnp.einsum("shqk,skhd->sqhd", score_grad_low, key_heads, preferred_element_type=jnp.float32) * DH ** (-0.5)
    key_grad = jnp.einsum("shqk,sqhd->skhd", score_grad_low, query_heads, preferred_element_type=jnp.float32) * DH ** (-0.5)
    query_grad_low = query_grad.reshape(token_count, H * DH).astype(low_type)
    key_grad_low = key_grad.reshape(token_count, H * DH).astype(low_type)
    value_grad_low = value_grad.reshape(token_count, H * DH).astype(low_type)
    grad_tokens = (grad_first + back_dot(query_grad_low, whole_query) + back_dot(key_grad_low, whole_key)
                   + back_dot(value_grad_low, whole_value))
    terms = (
        weight_term(token_low, query_grad_low),
        weight_term(token_low, key_grad_low),
        weight_term(token_low, value_grad_low),
        weight_term(context_low, branch_grad_low),
        weight_term(normed_low, hidden_grad_low),
        weight_term(activated_low, outer_grad_low),
    )
    vector_grads = (column_sum(query_grad_low), column_sum(value_grad_low), column_sum(branch_grad_low),
                    column_sum(hidden_grad_low), column_sum(outer_grad_low),
                    grad_scale_attn, grad_offset_attn, grad_scale_block, grad_offset_block)
    peak_rows = jnp.pad(local_top, (0, 1024 - H), constant_values=neg_fill)
    vec = vector_rows((*vector_grads, peak_rows))
    reduced = reduce_all(terms, vec, (5, 4, 3, 0, 1, 2))
    block_grads, vec_total = sum_groups(reduced[:6], reduced[6])

    at = lax.axis_index("row") * cols + lax.axis_index("col")
    owned, start = [], 0
    for n, whole_n in zip(lengths, spread):
        vector = vec_total[start : start + whole_n // 128].reshape(-1)
        owned.append(lax.dynamic_slice(vector, (at * n,), (n,)))
        start += whole_n // 128
    head_peak = vec_total[start, :H]
    tau_value = tau_num[0].astype(jnp.float32) / tau_den[0].astype(jnp.float32)
    factor = jnp.sqrt(tau_value / jnp.maximum(head_peak, tau_value))
    col_width = weight_query.shape[1]
    col_heads = (lax.axis_index("col") * col_width + jnp.arange(col_width, dtype=jnp.int32)) // DH
    column_factor = jnp.sum(
        jnp.where(col_heads[:, None] == jnp.arange(H, dtype=jnp.int32)[None, :], factor[None, :], 0.0), axis=1)
    return (output, grad_tokens, *block_grads, *owned, head_peak,
            weight_query * column_factor[None, :], weight_key * column_factor[None, :])


def sum_groups(blocks, vec):
    count = lax.axis_size("dp")
    totals, vec_sum = list(blocks), vec
    split = vec.shape[0] - 8
    for step in range(4, count, 4):
        shift = [(i, (i + step) % count) for i in range(count)]
        totals = [t + lax.ppermute(b, "dp", shift) for t, b in zip(totals, blocks)]
        moved = lax.ppermute(vec, "dp", shift)
        vec_sum = jnp.concatenate([vec_sum[:split] + moved[:split], jnp.maximum(vec_sum[split:], moved[split:])])
    return totals, vec_sum


def solution(mesh):
    tokens_spec, block_spec, vector_spec = P(("dp", "row", "col"), None), P("row", "col"), P(("row", "col"))
    in_specs = (tokens_spec, P(("dp", "row", "col")), tokens_spec, *(block_spec,) * 6, *(vector_spec,) * 9, P(), P())
    out_specs = (tokens_spec, tokens_spec, *(block_spec,) * 6, *(vector_spec,) * 9, P(), block_spec, block_spec)
    return jax.shard_map(on_device, mesh=mesh, in_specs=in_specs, out_specs=out_specs, check_vma=False)
```

time: 1240 us -> 517 us (0.42); the launches traced: 1220 us -> 514 us
  waiting for transfers between devices: 661 us -> 0 us
  Pallas kernels: 0 us -> 300 us
  blocking collectives: 219 us -> 0 us
  local copies, waits for them, and re-layouts: 123 us -> 28.7 us
  other arithmetic: 53.2 us -> 38 us
  between operations: 16.5 us -> 3.27 us
    reduce_scatter x6 -> x0, waiting for transfers between devices: 373 us -> none  [the longest x1 151 us: on_device(): lax.psum_scatter(terms[5].astype(jnp.bfloat16), ('row', 'col'), scatter_d...]
    pallas_call x0 -> x2, Pallas kernels: none -> 300 us  [the longest x1 170 us: reduce_all(): pl.pallas_call(functools.partial(reduce_kernel, rows, cols, entries), out...]
    all_gather x6 -> x0, waiting for transfers between devices: 228 us -> none  [the longest x1 106 us: fetch_params(): lax.all_gather(wire_items[4], ('row', 'col'), axis=0, tiled=True)]
    all_gather x9 -> x0, blocking collectives: 137 us -> none  [the longest x1 22.7 us: fetch_params(): lax.all_gather(wire_items[9], ('row', 'col'), axis=0, tiled=True)]
    reshape x15 -> x5, local copies, waits for them, and re-layouts: 66.7 us -> 2.32 us  [the longest x2 1.59 us: on_device(): vector = vec_total[start:start + whole_n // 128].reshape(-1)]
    psum x1 -> x0, waiting for transfers between devices: 59.9 us -> none  [on_device(): lax.psum(parted[0][0].astype(jnp.bfloat16), 'dp').astype(jnp.float32)]
    convert_element_type x18 -> x1, local copies, waits for them, and re-layouts: 46.9 us -> 0.54 us  [on_device(): context_grad_low = back_dot(branch_grad_low, whole_output).astype(low_type)]
    pmax x1 -> x0, blocking collectives: 39.5 us -> none  [on_device(): head_peak = lax.pmax(local_top, ('dp', 'row', 'col'))]
  transfers between devices with their start and end apart: 13 -> 0, of which waited for: 8 -> 0; matrix products, arithmetic and copies ran while one was open for 18% -> 0% of each run, Pallas kernels for 0% -> 0%
where the time goes in v1:
time: 517 us; the launch traced here: 514 us
  Pallas kernels  300 us (58%)
  matrix products  144 us (28%)
  other arithmetic  38 us (7%)
  local copies, waits for them, and re-layouts  28.7 us (6%)
    pallas_call x1, Pallas kernels, reduce_all(): pl.pallas_call(functools.partial(reduce_kernel, rows, cols, entries), out...  170 us
    pallas_call x1, Pallas kernels, gather_all(): pl.pallas_call(functools.partial(gather_kernel, rows, cols, entries, ahea...  130 us
    dot_general x6, matrix products, forward_dot(): return jnp.dot(operand, weight, preferred_element_type=jnp.float32)  40.8 us
    dot_general x6, matrix products, back_dot(): lax.dot_general(gradient, weight, (((1,), (1,)), ((), ())), preferred_ele...  32 us
    dot_general x6, matrix products, weight_term(): lax.dot_general(operand, gradient, (((0,), (0,)), ((), ())), preferred_el...  25 us
    unnamed x161, local copies, waits for them, and re-layouts  20.1 us
    dot_general x1, matrix products, on_device(): jnp.einsum('sqhd,skhd->shqk', context_grad_heads, value_heads, preferred_...  14.7 us
    convert_element_type x1, other arithmetic, on_device(): score_grad_low = score_grad.astype(low_type)  10.8 us

profile of v1, /device:TPU:5, one launch (start us, length us, event | category | flops | bytes accessed | tf_op | source)
XLA Modules:
  0.0 514.0 jit_solution(6544080619477337590)
XLA Ops:
  0.7 1.9 convert_element_type.269.refs_0_
  2.7 1.8 convert_element_type.270.refs_1_
  4.5 1.8 convert_element_type.271.refs_2_
  6.3 1.8 convert_element_type.272.refs_3_
  8.1 1.1 convert_element_type.273.refs_4_
  9.2 1.1 convert_element_type.274.refs_5_
  13.3 129.9 %gather_all.1 = (bf16[1024,1024]{1,0:T(8,128)(2,1)}, bf16[1024,1024]{1,0:T(8,128)(2,1)}, bf16[1024,1024]{1,0:T(8,128)(2,1)}, bf16[1024,1024]{1,0:T(8,128)(2,1)},...) custom-call(bf16[512,256]{1,0:T(8,128)(2,1)} %convert_element_type.269.refs_0_, ...), custom_call_target="tpu_custom_call" | custom-call | tf_op jit(solution)/shard_map/gather_all/pallas_call | solution.py:217
  144.2 3.3 add_convert_fusion.2
  147.6 1.3 add_convert_fusion.1
  149.5 1.6 convolution_convert_fusion.4
  151.3 7.4 %fusion.34 = (f32[16,512]{1,0:T(8,128)S(1)}, f32[16,512,512]{1,2,0:T(8,128)}) fusion(bf16[512,16,64]{0,2,1:T(8,128)(2,1)S(1)} %bitcast.174, bf16[512,16,64]{0,2,1:T(8,128)(2,1)S(1)} %bitcast.172, pred[512,512]{0,1:T(8,128)(4,1)S(1)} %broadcast_compare_fusion), kind=kOutput, calls=%fused_computation.128 | convolution fusion | flops 549445632 | bytes 19169280 | tf_op jit(solution)/shard_map/sqhd,skhd->shqk/dot_general | solution.py:502
  158.8 8.3 %fusion = f32[16,512]{1,0:T(8,128)S(1)} fusion(f32[16,512,512]{1,2,0:T(8,128)} %get-tuple-element.90, f32[16,512]{1,0:T(8,128)S(1)} %get-tuple-element.89), kind=kLoop, calls=%fused_computation.6 | loop fusion | flops 8380416 | bytes 16842752 | tf_op jit(solution)/shard_map/reduce_sum | solution.py:550
  167.1 7.7 %fusion.13 = bf16[16,64,512]{2,1,0:T(8,128)(2,1)S(1)} fusion(bf16[512,16,64]{0,2,1:T(8,128)(2,1)S(1)} %bitcast.180, f32[16,512,512]{1,2,0:T(8,128)} %get-tuple-element.90, f32[16,512]{1,0:T(8,128)S(1)} %fusion, f32[16,512]{1,0:T(8,128)S(1)} %get-tuple-element.89), kind=kOutput, calls=%fused_computation.60 | convolution fusion | flops 549978112 | bytes 18939904 | tf_op jit(solution)/shard_map/shqk,skhd->sqhd/dot_general | solution.py:553
  174.8 1.4 fusion.35
  176.6 28.5 %multiply_convert_fusion.1 = (bf16[512,4096]{1,0:T(8,128)(2,1)S(1)}, f32[512,4096]{1,0:T(8,128)}, f32[512,4096]{1,0:T(8,128)}) fusion(f32[4096]{0:T(1024)S(1)} %bitcast.187, bf16[1024,4096]{1,0:T(8,128)(2,1)} %get-tuple-element.39, f32[512,1024]{1,0:T(8,128)S(1)} %get-tuple-element.92, f32[1024]{0:T(1024)S(1)} %get-tuple-element.82, ...), kind=kOutput, calls=%fused_computation.14 | convolution fusion | flops 4436000768 | bytes 31485952 | tf_op jit(solution)/shard_map/dot_general | solution.py:485
  205.1 4.8 fusion.36
  210.3 1.4 multiply_reduce_fusion.1
  211.7 2.2 fusion.32
  214.7 15.7 %convert_reduce_fusion = (f32[4096]{0:T(1024)}, bf16[512,4096]{1,0:T(8,128)(2,1)}) fusion(f32[512,4096]{1,0:T(8,128)} %get-tuple-element.67, f32[512,4096]{1,0:T(8,128)} %get-tuple-element.93, f32[4096]{0:T(1024)S(1)} %bitcast.188, bf16[512,1024]{1,0:T(8,128)(2,1)S(1)} %get-tuple-element.57, bf16[4096,1024]{1,0:T(8,128)(2,1)} %get-tuple-element.40), kind=kOutput, calls=%fused_computation.11 | convolution fusion | flops 4330614784 | bytes 30441472 | tf_op jit(solution)/shard_map/dot_general | solution.py:489
  230.4 9.5 %multiply_reduce_fusion.2 = (f32[1024]{0:T(1024)}, f32[512]{0:T(512)S(1)}, f32[1024]{0:T(1024)}, f32[512,1024]{1,0:T(8,128)S(1)}) fusion(f32[512,1024]{1,0:T(8,128)S(1)} %get-tuple-element.92, f32[512]{0:T(512)S(1)} %fusion.25, f32[512]{0:T(512)S(1)} %broadcast_multiply_fusion.3, f32[1024]{0:T(1024)S(1)} %get-tuple-element.83, ...), kind=kOutput, calls=%fused_computation.34 | convolution fusion | flops 4300207616 | bytes 18894848 | tf_op jit(solution)/shard_map/dot_general | solution.py:489
  240.6 1.3 copy-done.1
  242.8 1.0 copy-done.23
  243.8 1.3 convolution_convert_fusion.3
  245.7 14.7 %fusion.30 = (f32[16]{0:T(128)}, f32[16,512]{1,0:T(8,128)}, f32[16,512,512]{1,2,0:T(8,128)}) fusion(f32[16,512,512]{1,2,0:T(8,128)} %get-tuple-element.90, f32[16,512]{1,0:T(8,128)} %log_add_fusion, bf16[512,16,64]{0,2,1:T(8,128)(2,1)S(1)} %bitcast.170, bf16[512,16,64]{0,2,1:T(8,128)(2,1)} %bitcast.181), kind=kOutput, calls=%fused_computation.125 | convolution fusion | flops 553639936 | bytes 35717184 | tf_op jit(solution)/shard_map/sqhd,skhd->shqk/dot_general | solution.py:575
  261.2 1.2 slice-done.3
  262.4 10.8 %multiply_convert_fusion = bf16[16,512,512]{1,2,0:T(8,128)(2,1)} fusion(f32[16,512,512]{1,2,0:T(8,128)} %get-tuple-element.97, f32[16,512,512]{1,2,0:T(8,128)S(1)} %bitcast.169, f32[16,512]{1,0:T(8,128)} %get-tuple-element.49, f32[16,512]{1,0:T(8,128)} %log_add_fusion), kind=kLoop, calls=%fused_computation | loop fusion | flops 16777216 | bytes 42008576 | tf_op jit(solution)/shard_map/convert_element_type | solution.py:577
  273.3 6.2 %multiply_convert_fusion.2 = bf16[16,64,512]{2,1,0:T(8,128)(2,1)S(1)} fusion(bf16[512,16,64]{0,2,1:T(8,128)(2,1)S(1)} %bitcast.175, bf16[16,512,512]{1,2,0:T(8,128)(2,1)} %multiply_convert_fusion), kind=kOutput, calls=%fused_computation.43 | convolution fusion | flops 537919488 | bytes 10485760 | tf_op jit(solution)/shard_map/shqk,sqhd->skhd/dot_general | solution.py:579
  279.5 1.3 fusion.38
  280.8 2.1 copy-done
  283.1 1.5 convert_reduce_fusion.4
  284.6 1.3 fusion.37
  286.0 8.8 %convert_reduce_fusion.3 = (f32[16,64]{1,0:T(8,128)S(1)}, bf16[16,64,512]{2,1,0:T(8,128)(2,1)S(1)}) fusion(bf16[512,16,64]{0,2,1:T(8,128)(2,1)S(1)} %bitcast.171, f32[16,512,512]{1,2,0:T(8,128)} %get-tuple-element.90, f32[16,512]{1,0:T(8,128)S(1)} %copy-done.25), kind=kOutput, calls=%fused_computation.37 | convolution fusion | flops 546831360 | bytes 18911232 | tf_op jit(solution)/shard_map/shqk,sqhd->skhd/dot_general | solution.py:574
  294.8 3.0 add_add_fusion.2
  297.7 2.6 convert_bitcast_fusion.2.refs_0_
  300.4 2.6 convert_bitcast_fusion.1.refs_1_
  303.0 3.0 convert_bitcast_fusion.refs_2_
  306.0 2.6 convolution_convert_fusion.2.refs_3_
  308.6 1.0 copy-done.61
  309.6 7.4 %convolution_convert_fusion.1.refs_4_ = bf16[1024,4096]{1,0:T(8,128)(2,1)} fusion(bf16[512,4096]{1,0:T(8,128)(2,1)S(1)} %copy-done.61, f32[512,1024]{1,0:T(8,128)S(1)} %copy-done.4, f32[1024]{0:T(1024)S(1)} %copy-done.39, f32[1024]{0:T(1024)S(1)} %copy-done.32, f32[512]{0:T(512)S(1)} %copy-done.37, f32[512]{0:T(512)S(1)} %broadcast_multiply_fusion.3), kind=kOutput, calls=%fused_computation.30 | convolution fusion | flops 4301783040 | bytes 14692352 | tf_op jit(solution)/shard_map/dot_general | solution.py:493
  317.1 6.8 %convolution_convert_fusion.refs_5_ = bf16[4096,1024]{1,0:T(8,128)(2,1)} fusion(bf16[512,4096]{1,0:T(8,128)(2,1)S(1)} %copy-done.60, bf16[512,1024]{1,0:T(8,128)(2,1)S(1)} %copy-done.22), kind=kOutput, calls=%fused_computation.29 | convolution fusion | flops 4299161600 | bytes 13631488 | tf_op jit(solution)/shard_map/dot_general | solution.py:493
  324.8 170.1 %reduce_all.1 = (f32[512,256]{1,0:T(8,128)}, f32[512,256]{1,0:T(8,128)}, f32[512,256]{1,0:T(8,128)}, f32[512,256]{1,0:T(8,128)}, f32[512,1024]{1,0:T(8,128)}, /*index=5*/f32[2048,256]{1,0:T(8,128)}, f32[104,128]{1,0:T(8,128)}) custom-call(bf16[1024,1024]{1,0:T(8,128)(2,1)} %convert_bitcast_fusion.2.refs_0_, ...), custom_call_target="tpu_custom_call" | custom-call | tf_op jit(solution)/shard_map/reduce_all/pallas_call | solution.py:458
  494.9 0.9 slice_bitcast_fusion.1
  503.1 1.2 sqrt_bitcast_fusion
  504.4 1.0 broadcast_multiply_fusion
  505.5 2.0 copy.102
  507.5 1.9 copy.103
  510.9 1.3 copy.106
  512.3 1.3 copy.107
  (200 shorter events, 18.4 us)
Async XLA Ops:
  0.7 7.4 %copy-start.10 = (f32[512,1024]{1,0:T(8,128)S(1)}, f32[512,1024]{1,0:T(8,128)}, u32[]{:S(2)}) copy-start(f32[512,1024]{1,0:T(8,128)} %param.27) | copy-start | bytes 6291460
  0.7 8.5 %copy-start.11 = (f32[2048,256]{1,0:T(8,128)S(1)}, f32[2048,256]{1,0:T(8,128)}, u32[]{:S(2)}) copy-start(f32[2048,256]{1,0:T(8,128)} %param.28) | copy-start | bytes 6291460
  2.6 7.7 %copy-start.49 = (f32[128]{0:T(128)S(1)}, f32[128]{0:T(128)}, u32[]{:S(2)}) copy-start(f32[128]{0:T(128)} %param.29) | copy-start | bytes 1540
  2.6 7.9 %copy-start.50 = (f32[128]{0:T(128)S(1)}, f32[128]{0:T(128)}, u32[]{:S(2)}) copy-start(f32[128]{0:T(128)} %param.30) | copy-start | bytes 1540
  2.6 8.1 %copy-start.51 = (f32[128]{0:T(128)S(1)}, f32[128]{0:T(128)}, u32[]{:S(2)}) copy-start(f32[128]{0:T(128)} %param.31) | copy-start | bytes 1540
  2.6 8.4 %copy-start.43 = (f32[512]{0:T(512)S(1)}, f32[512]{0:T(512)}, u32[]{:S(2)}) copy-start(f32[512]{0:T(512)} %param.32) | copy-start | bytes 6148
  2.6 8.6 %copy-start.52 = (f32[128]{0:T(128)S(1)}, f32[128]{0:T(128)}, u32[]{:S(2)}) copy-start(f32[128]{0:T(128)} %param.33) | copy-start | bytes 1540
  2.6 8.9 %copy-start.53 = (f32[128]{0:T(128)S(1)}, f32[128]{0:T(128)}, u32[]{:S(2)}) copy-start(f32[128]{0:T(128)} %param.34) | copy-start | bytes 1540
  2.6 9.1 %copy-start.54 = (f32[128]{0:T(128)S(1)}, f32[128]{0:T(128)}, u32[]{:S(2)}) copy-start(f32[128]{0:T(128)} %param.35) | copy-start | bytes 1540
  2.6 9.3 %copy-start.55 = (f32[128]{0:T(128)S(1)}, f32[128]{0:T(128)}, u32[]{:S(2)}) copy-start(f32[128]{0:T(128)} %param.36) | copy-start | bytes 1540
  2.7 9.6 %copy-start.56 = (f32[128]{0:T(128)S(1)}, f32[128]{0:T(128)}, u32[]{:S(2)}) copy-start(f32[128]{0:T(128)} %param.37) | copy-start | bytes 1540
  8.1 135.9 %copy-start.12 = (f32[512,1024]{1,0:T(8,128)S(1)}, f32[512,1024]{1,0:T(8,128)}, u32[]{:S(2)}) copy-start(f32[512,1024]{1,0:T(8,128)} %param.20) | copy-start | bytes 6291460
  144.0 61.1 %copy-start.38 = (f32[1024]{0:T(1024)}, f32[1024]{0:T(1024)S(1)}, u32[]{:S(2)}) copy-start(f32[1024]{0:T(1024)S(1)} %get-tuple-element.82) | copy-start | bytes 12292
  144.0 95.9 %copy-start.31 = (f32[1024]{0:T(1024)}, f32[1024]{0:T(1024)S(1)}, u32[]{:S(2)}) copy-start(f32[1024]{0:T(1024)S(1)} %get-tuple-element.83) | copy-start | bytes 12292
  144.2 4.7 copy-start.18
  147.5 19.5 %copy-start.20 = (bf16[1024,512]{1,0:T(8,128)(2,1)}, bf16[1024,512]{1,0:T(8,128)(2,1)S(1)}, u32[]{:S(2)}) copy-start(bf16[1024,512]{1,0:T(8,128)(2,1)S(1)} %add_convert_fusion.2) | copy-start | bytes 3145732
  151.1 7.7 %copy-start.6 = (bf16[1024,512]{1,0:T(8,128)(2,1)}, bf16[1024,512]{1,0:T(8,128)(2,1)S(1)}, u32[]{:S(2)}) copy-start(bf16[1024,512]{1,0:T(8,128)(2,1)S(1)} %convolution_convert_fusion.4) | copy-start | bytes 3145732
  167.1 7.7 %copy-start.48 = (bf16[1024,1024]{1,0:T(8,128)(2,1)S(1)}, bf16[1024,1024]{1,0:T(8,128)(2,1)}, u32[]{:S(2)}) copy-start(bf16[1024,1024]{1,0:T(8,128)(2,1)} %get-tuple-element.38) | copy-start | bytes 6291460
  174.8 30.3 %slice-start.4 = ((s8[8388608]{0:T(1024)(128)(4,1)}), s8[4194304]{0:T(1024)(128)(4,1)S(1)}, s32[]{:S(2)}) async-start(s8[8388608]{0:T(1024)(128)(4,1)} %bitcast.189), calls=%async_computation.4 | async-start | bytes 8388608
  176.2 63.7 %copy-start.3 = (f32[512,1024]{1,0:T(8,128)}, f32[512,1024]{1,0:T(8,128)S(1)}, u32[]{:S(2)}) copy-start(f32[512,1024]{1,0:T(8,128)S(1)} %get-tuple-element.92) | copy-start | bytes 6291460
  176.6 63.3 %copy-start.36 = (f32[512]{0:T(512)}, f32[512]{0:T(512)S(1)}, u32[]{:S(2)}) copy-start(f32[512]{0:T(512)S(1)} %fusion.25) | copy-start | bytes 6148
  176.6 28.5 %slice-start.5 = ((s8[8388608]{0:T(1024)(128)(4,1)}), s8[4194304]{0:T(1024)(128)(4,1)S(1)}, s32[]{:S(2)}) async-start(s8[8388608]{0:T(1024)(128)(4,1)} %bitcast.189), calls=%async_computation.5 | async-start | bytes 8388608
  205.1 4.8 copy-start.59
  205.1 5.1 %copy-start.5 = (f32[512,1024]{1,0:T(8,128)S(1)}, f32[512,1024]{1,0:T(8,128)}, u32[]{:S(2)}) copy-start(f32[512,1024]{1,0:T(8,128)} %param.22) | copy-start | bytes 6291460
  214.7 15.7 %copy-start.21 = (bf16[512,1024]{1,0:T(8,128)(2,1)}, bf16[512,1024]{1,0:T(8,128)(2,1)S(1)}, u32[]{:S(2)}) copy-start(bf16[512,1024]{1,0:T(8,128)(2,1)S(1)} %get-tuple-element.57) | copy-start | bytes 3145732
  245.6 14.8 %slice-start = ((s8[16777216]{0:T(1024)(128)(4,1)}), s8[4194304]{0:T(1024)(128)(4,1)S(1)}, s32[]{:S(2)}) async-start(s8[16777216]{0:T(1024)(128)(4,1)} %bitcast.168), calls=%async_computation | async-start | bytes 8388608
  245.6 14.7 %slice-start.1 = ((s8[16777216]{0:T(1024)(128)(4,1)}), s8[4194304]{0:T(1024)(128)(4,1)S(1)}, s32[]{:S(2)}) async-start(s8[16777216]{0:T(1024)(128)(4,1)} %bitcast.168), calls=%async_computation.1 | async-start | bytes 8388608
  245.6 15.6 %slice-start.2 = ((s8[16777216]{0:T(1024)(128)(4,1)}), s8[4194304]{0:T(1024)(128)(4,1)S(1)}, s32[]{:S(2)}) async-start(s8[16777216]{0:T(1024)(128)(4,1)} %bitcast.168), calls=%async_computation.2 | async-start | bytes 8388608
  245.6 16.8 %slice-start.3 = ((s8[16777216]{0:T(1024)(128)(4,1)}), s8[4194304]{0:T(1024)(128)(4,1)S(1)}, s32[]{:S(2)}) async-start(s8[16777216]{0:T(1024)(128)(4,1)} %bitcast.168), calls=%async_computation.3 | async-start | bytes 8388608
  262.4 10.9 %copy-start.9 = (bf16[1024,512]{1,0:T(8,128)(2,1)S(1)}, bf16[1024,512]{1,0:T(8,128)(2,1)}, u32[]{:S(2)}) copy-start(bf16[1024,512]{1,0:T(8,128)(2,1)} %copy-done.8) | copy-start | bytes 3145732
  273.3 6.2 %copy-start.47 = (bf16[1024,1024]{1,0:T(8,128)(2,1)S(1)}, bf16[1024,1024]{1,0:T(8,128)(2,1)}, u32[]{:S(2)}) copy-start(bf16[1024,1024]{1,0:T(8,128)(2,1)} %get-tuple-element.37) | copy-start | bytes 6291460
  286.0 8.8 %copy-start.2 = (f32[512,1024]{1,0:T(8,128)S(1)}, f32[512,1024]{1,0:T(8,128)}, u32[]{:S(2)}) copy-start(f32[512,1024]{1,0:T(8,128)} %copy-done.1) | copy-start | bytes 6291460
  286.0 8.8 %copy-start.17 = (bf16[1024,1024]{1,0:T(8,128)(2,1)S(1)}, bf16[1024,1024]{1,0:T(8,128)(2,1)}, u32[]{:S(2)}) copy-start(bf16[1024,1024]{1,0:T(8,128)(2,1)} %get-tuple-element.34) | copy-start | bytes 6291460
  309.6 7.4 %copy-start.22 = (bf16[512,1024]{1,0:T(8,128)(2,1)S(1)}, bf16[512,1024]{1,0:T(8,128)(2,1)}, u32[]{:S(2)}) copy-start(bf16[512,1024]{1,0:T(8,128)(2,1)} %copy-done.21) | copy-start | bytes 3145732
  309.6 7.4 %copy-start.60 = (bf16[512,4096]{1,0:T(8,128)(2,1)S(1)}, bf16[512,4096]{1,0:T(8,128)(2,1)}, u32[]{:S(2)}) copy-start(bf16[512,4096]{1,0:T(8,128)(2,1)} %copy-done.59) | copy-start | bytes 12582916
  317.0 7.0 %copy-start.29 = (f32[1024]{0:T(1024)S(1)}, f32[1024]{0:T(1024)}, u32[]{:S(2)}) copy-start(f32[1024]{0:T(1024)} %get-tuple-element.60) | copy-start | bytes 12292
  317.0 7.0 %copy-start.30 = (f32[4096]{0:T(1024)S(1)}, f32[4096]{0:T(1024)}, u32[]{:S(2)}) copy-start(f32[4096]{0:T(1024)} %get-tuple-element.58) | copy-start | bytes 49156
  317.0 7.0 %copy-start.41 = (f32[1024]{0:T(1024)S(1)}, f32[1024]{0:T(1024)}, u32[]{:S(2)}) copy-start(f32[1024]{0:T(1024)} %get-tuple-element.52) | copy-start | bytes 12292
  317.0 7.0 %copy-start.40 = (f32[1024]{0:T(1024)S(1)}, f32[1024]{0:T(1024)}, u32[]{:S(2)}) copy-start(f32[1024]{0:T(1024)} %get-tuple-element.55) | copy-start | bytes 12292
  317.0 7.1 %copy-start.34 = (f32[1024]{0:T(1024)S(1)}, f32[1024]{0:T(1024)}, u32[]{:S(2)}) copy-start(f32[1024]{0:T(1024)} %get-tuple-element.50) | copy-start | bytes 12292
  317.1 7.1 %copy-start.33 = (f32[1024]{0:T(1024)S(1)}, f32[1024]{0:T(1024)}, u32[]{:S(2)}) copy-start(f32[1024]{0:T(1024)} %get-tuple-element.54) | copy-start | bytes 12292
  317.1 7.1 %copy-start.42 = (f32[16]{0:T(128)S(1)}, f32[16]{0:T(128)}, u32[]{:S(2)}) copy-start(f32[16]{0:T(128)} %get-tuple-element.48) | copy-start | bytes 196
  324.8 179.6 %copy-start.15 = (f32[512,256]{1,0:T(8,128)S(1)}, f32[512,256]{1,0:T(8,128)}, u32[]{:S(2)}) copy-start(f32[512,256]{1,0:T(8,128)} %param.23) | copy-start | bytes 1572868
  324.8 179.6 %copy-start.16 = (f32[512,256]{1,0:T(8,128)S(1)}, f32[512,256]{1,0:T(8,128)}, u32[]{:S(2)}) copy-start(f32[512,256]{1,0:T(8,128)} %param.24) | copy-start | bytes 1572868
  494.9 16.1 %copy-start.14 = (f32[512,1024]{1,0:T(8,128)S(1)}, f32[512,1024]{1,0:T(8,128)}, u32[]{:S(2)}) copy-start(f32[512,1024]{1,0:T(8,128)} %get-tuple-element.128) | copy-start | bytes 6291460
  504.3 5.0 copy-start.27
  504.3 5.8 %copy-start.26 = (f32[512,256]{1,0:T(8,128)S(1)}, f32[512,256]{1,0:T(8,128)}, u32[]{:S(2)}) copy-start(f32[512,256]{1,0:T(8,128)} %get-tuple-element.127) | copy-start | bytes 1572868
  505.5 6.8 %copy-start.13 = (f32[2048,256]{1,0:T(8,128)S(1)}, f32[2048,256]{1,0:T(8,128)}, u32[]{:S(2)}) copy-start(f32[2048,256]{1,0:T(8,128)} %get-tuple-element.129) | copy-start | bytes 6291460
  (20 other events, 46.6 us)

commit v2 on v1

--- a/solution.py
+++ b/solution.py
@@ -8,8 +8,11 @@
 
 MESH = pl.DeviceIdType.MESH
 
-LAGS = (0, 2, 5, 60)
+LAGS = (0, 2, 5)
 SEQ, H, DH = 512, 16, 64
+norm_eps = 1e-12
+neg_fill = -1e30
+low_type = jnp.bfloat16
 
 def place():
     dp = lax.axis_index("dp")
@@ -76,67 +79,82 @@
     return found
 
 
-def gather_kernel(rows, cols, entries, ahead, *refs):
-    count = 1 + max(entry[0] for entry in entries)
-    number = len(entries)
-    blocks, vec = refs[:count], refs[count]
-    wholes, vecs = refs[count + 1 : 2 * count + 1], refs[2 * count + 1]
-    (z_in, x_in, y_in, c_in, v_in, z_out, x_out, y_out, c_out, v_out, own_sem, own_vec) = refs[2 * count + 2 :]
+def assemble_vectors(vecs, full_vec, lengths):
+    groups = vecs.shape[0]
+    for d in range(groups):
+        rows_of = vecs[d].astype(jnp.float32)
+        at = 0
+        for i, n in enumerate(lengths):
+            for part in range(-(-n // 128)):
+                width = min(128, n - part * 128)
+                start = d * n + part * 128
+                full_vec[i : i + 1, start : start + width] = rows_of[at : at + 1, :width]
+                at += 1
+
+
+def row_stats(values):
+    center = values - jnp.mean(values, axis=-1, keepdims=True)
+    spread = jnp.mean(center * center, axis=-1, keepdims=True)
+    scale = lax.rsqrt(spread + norm_eps)
+    return center * scale, scale
+
+
+def forward_kernel(rows, cols, entries, lengths, ahead, *refs):
+    refs = list(refs)
+    take = lambda n: [refs.pop(0) for _ in range(n)]
+    blocks = take(6)
+    vec, tokens, cotangent, seg_col, seg_row = take(5)
+    wholes_out = take(6)
+    (full_vec, q, k, v, ctx, stat, peak, n1, h1r, g, gp, output, dz2, sums) = take(14)
+    wholes = take(6)
+    vecs, token_low = take(2)
+    (z_in, x_in, y_in, c_in, v_in, z_out, x_out, y_out, c_out, v_out, out_sem, own_vec) = refs
+    count, number = 6, len(entries)
     row, col, dp, core, side = place()
+    other = 1 - row
+    mine = row * cols + col
+    x_dev, y_dev, c_dev = {"row": other}, y_peer(dp), core_peer(dp)
+    sends = Sends()
+
+    for m in range(count):
+        height, width = blocks[m].shape
+        step = 32768 // width
+        to_col = pl.ds(pl.multiple_of(col * width, width), width)
+
+        @pl.loop(0, height // step)
+        def _(i):
+            wholes[m][pl.ds(pl.multiple_of(row * height + i * step, step), step), to_col] = (
+                blocks[m][pl.ds(pl.multiple_of(i * step, step), step), :].astype(low_type))
+
     group_barrier(rows, cols)
-    sends = Sends()
-    other = 1 - row
-    x_dev, y_dev, c_dev = {"row": other}, y_peer(dp), core_peer(dp)
-    mine = row * cols + col
-
     for step in range(1, rows * cols):
         peer = (mine + step) % (rows * cols)
-        sends.start(None, vec, vecs.at[mine], v_out.at[step], v_in.at[mine],
-                    {"row": peer // cols, "col": peer % cols})
-
-    def offset(e, of_core, of_side):
-        _, paired, base, part = entries[e]
-        return base + ((of_core * 2 + of_side) * part if paired else of_core * part)
+        sends.start(None, vec, vecs.at[mine], v_out.at[step], v_in.at[mine], {"row": peer // cols, "col": peer % cols})
 
     def region(e, of_row, of_col, of_core, of_side):
-        m, _, _, part = entries[e]
+        m, paired, base, part = entries[e]
         height, width = blocks[m].shape
-        start = of_row * height + offset(e, of_core, of_side)
-        return wholes[m].at[pl.ds(pl.multiple_of(start, 16), part),
-                            pl.ds(pl.multiple_of(of_col * width, width), width)]
-
-    def own_part(e):
-        m, _, _, part = entries[e]
-        return blocks[m].at[pl.ds(pl.multiple_of(offset(e, core, side), 16), part), :]
+        start = of_row * height + base + ((of_core * 2 + of_side) * part if paired else of_core * part)
+        return wholes[m].at[pl.ds(pl.multiple_of(start, 16), part), pl.ds(pl.multiple_of(of_col * width, width), width)]
 
     def send_own(e):
-        dst = region(e, row, col, core, side)
-        src = own_part(e)
+        piece = region(e, row, col, core, side)
         for step in range(1, cols):
-            sends.start(col + step < cols, src, dst, z_out.at[e, step, 0], z_in.at[e, col], {"col": jnp.minimum(col + step, cols - 1)})
-            sends.start(col >= step, src, dst, z_out.at[e, step, 1], z_in.at[e, col], {"col": jnp.maximum(col - step, 0)})
+            sends.start(col + step < cols, piece, piece, z_out.at[e, step, 0], z_in.at[e, col], {"col": jnp.minimum(col + step, cols - 1)})
+            sends.start(col >= step, piece, piece, z_out.at[e, step, 1], z_in.at[e, col], {"col": jnp.maximum(col - step, 0)})
             if step == 1:
-                sends.start(None, src, dst, x_out.at[e, col], x_in.at[e, col], x_dev)
-
-    def keep_own(m):
-        height, width = blocks[m].shape
-        return pltpu.make_async_copy(
-            blocks[m],
-            wholes[m].at[pl.ds(pl.multiple_of(row * height, height), height),
-                         pl.ds(pl.multiple_of(col * width, width), width)],
-            own_sem.at[m])
-
-    def share(m, of_row, of_col, when):
-        piece = region(m, of_row, of_col, core, side)
-        if entries[m][1]:
-            sends.start(when, piece, piece, y_out.at[m, of_row, of_col], y_in.at[m, of_row, of_col], y_dev)
-        sends.start(when, piece, piece, c_out.at[m, of_row, of_col, 0], c_in.at[m, of_row, of_col, 0], c_dev)
+                sends.start(None, piece, piece, x_out.at[e, col], x_in.at[e, col], x_dev)
+
+    def share(e, of_row, of_col, when):
+        piece = region(e, of_row, of_col, core, side)
+        if entries[e][1]:
+            sends.start(when, piece, piece, y_out.at[e, of_row, of_col], y_in.at[e, of_row, of_col], y_dev)
+        sends.start(when, piece, piece, c_out.at[e, of_row, of_col, 0], c_in.at[e, of_row, of_col, 0], c_dev)
 
     def columns(step):
         if step == 0:
-            return [(0, None, col)]
-        return [(-1, col >= step, jnp.maximum(col - step, 0)),
-                (1, col + step < cols, jnp.minimum(col + step, cols - 1))]
+            return [(None, col)]
+        return [(col >= step, jnp.maximum(col - step, 0)), (col + step < cols, jnp.minimum(col + step, cols - 1))]
 
     def guarded(when, body):
         if when is None:
@@ -144,89 +162,226 @@
         else:
             pl.when(when)(body)
 
-    def both(a, b):
-        return b if a is None else jnp.logical_and(a, b)
-
-    def z_stage(m, step):
+    def z_stage(e, step):
         if step == 0:
-            if m + ahead < number:
-                send_own(m + ahead)
+            if e + ahead < number:
+                send_own(e + ahead)
             return
-        for sign, when, at in columns(step):
-            piece = region(m, row, at, core, side)
-            guarded(when, lambda: wait_arrival(piece, z_in.at[m, at], {"col": col}))
-            sends.start(when, piece, piece, x_out.at[m, at], x_in.at[m, at], x_dev)
-            share(m, row, at, when)
-
-    def x_stage(m, step):
-        for _, when, at in columns(step):
-            piece = region(m, other, at, core, side)
-            guarded(when, lambda: wait_arrival(piece, x_in.at[m, at], x_dev))
-            share(m, other, at, when)
-
-    def y_stage(m, step):
-        if not entries[m][1]:
+        for when, at in columns(step):
+            piece = region(e, row, at, core, side)
+            guarded(when, lambda: wait_arrival(piece, z_in.at[e, at], {"col": col}))
+            sends.start(when, piece, piece, x_out.at[e, at], x_in.at[e, at], x_dev)
+            share(e, row, at, when)
+
+    def x_stage(e, step):
+        for when, at in columns(step):
+            piece = region(e, other, at, core, side)
+            guarded(when, lambda: wait_arrival(piece, x_in.at[e, at], x_dev))
+            share(e, other, at, when)
+
+    def y_stage(e, step):
+        if not entries[e][1]:
             return
-        for _, when, at in columns(step):
+        for when, at in columns(step):
             for of_row in (row, other):
                 if step == 0 and of_row is row:
                     continue
-                piece = region(m, of_row, at, core, 1 - side)
-                guarded(when, lambda: wait_arrival(piece, y_in.at[m, of_row, at], y_dev))
-                sends.start(when, piece, piece, c_out.at[m, of_row, at, 1], c_in.at[m, of_row, at, 1], c_dev)
-
-    def c_stage(m, step):
-        for _, when, at in columns(step):
+                piece = region(e, of_row, at, core, 1 - side)
+                guarded(when, lambda: wait_arrival(piece, y_in.at[e, of_row, at], y_dev))
+                sends.start(when, piece, piece, c_out.at[e, of_row, at, 1], c_in.at[e, of_row, at, 1], c_dev)
+
+    def c_stage(e, step):
+        for when, at in columns(step):
             for of_row in (row, other):
                 if step == 0 and of_row is row:
                     continue
-                piece = region(m, of_row, at, 1 - core, side)
-                guarded(when, lambda: wait_arrival(piece, c_in.at[m, of_row, at, 0], c_dev))
-                if entries[m][1]:
-                    far = region(m, of_row, at, 1 - core, 1 - side)
-                    guarded(when, lambda: wait_arrival(far, c_in.at[m, of_row, at, 1], c_dev))
+                piece = region(e, of_row, at, 1 - core, side)
+                guarded(when, lambda: wait_arrival(piece, c_in.at[e, of_row, at, 0], c_dev))
+                if entries[e][1]:
+                    far = region(e, of_row, at, 1 - core, 1 - side)
+                    guarded(when, lambda: wait_arrival(far, c_in.at[e, of_row, at, 1], c_dev))
+
+    def keep(m):
+        return pltpu.make_async_copy(wholes[m], wholes_out[m], out_sem.at[m])
+
+    def complete(m):
+        for e in range(number):
+            if entries[e][0] == m:
+                for step in range(cols):
+                    c_stage(e, step)
+        keep(m).start()
+
+    tokens_count = tokens.shape[0]
+
+    def cast_tokens():
+        @pl.loop(0, tokens_count // 64)
+        def _(i):
+            at = pl.ds(pl.multiple_of(i * 64, 64), 64)
+            token_low[at, :] = tokens[at, :].astype(low_type)
+
+    def finish_vectors():
+        for step in range(1, rows * cols):
+            peer = (mine + step) % (rows * cols)
+            wait_arrival(vecs.at[peer], v_in.at[peer], {"row": peer // cols, "col": peer % cols})
+        keep_vec.wait()
+        assemble_vectors(vecs, full_vec, lengths)
+
+    def project(m, into, bias):
+        @pl.loop(0, into.shape[1] // 256)
+        def _(j):
+            at = pl.ds(pl.multiple_of(j * 256, 256), 256)
+            total = jnp.dot(token_low[...], wholes[m][:, at], preferred_element_type=jnp.float32)
+            if bias is not None:
+                total = total + full_vec[bias : bias + 1, at]
+            into[:, at] = total.astype(low_type)
+
+    def start_attention():
+        stat[...] = jnp.zeros_like(stat)
+        peak[...] = jnp.full(peak.shape, neg_fill, jnp.float32)
+
+    def attend(pair, half):
+        lanes = slice(pair * 128, pair * 128 + 128)
+        lane = lax.broadcasted_iota(jnp.int32, (1, 128), 1)
+        place_of = lax.broadcasted_iota(jnp.int32, (128, 128), 1)
+        peak_place = lax.broadcasted_iota(jnp.int32, peak.shape, 1)
+
+        @pl.loop(half * 2, half * 2 + 2)
+        def _(i):
+            at = pl.ds(pl.multiple_of(i * 128, 128), 128)
+            same = seg_col[at, :] == seg_row[...]
+            parts = []
+            for a in range(2):
+                head = 2 * pair + a
+                keep_lanes = jnp.where((lane < 64) == (a == 0), DH ** (-0.5), 0.0).astype(low_type)
+                scores = lax.dot_general(q[at, lanes] * keep_lanes, k[:, lanes], (((1,), (1,)), ((), ())),
+                                         preferred_element_type=jnp.float32)
+                scores = jnp.where(same, scores, neg_fill)
+                top = jnp.max(scores, axis=1, keepdims=True)
+                raised = jnp.exp(scores - top)
+                total = jnp.sum(raised, axis=1, keepdims=True)
+                attend_low = (raised * (1.0 / total)).astype(low_type)
+                parts.append(jnp.dot(attend_low, v[:, lanes], preferred_element_type=jnp.float32))
+                stat[at, :] = jnp.where(place_of == head, top + jnp.log(total), stat[at, :])
+                peak[...] = jnp.where(peak_place == head, jnp.maximum(peak[...], jnp.max(top, axis=0, keepdims=True)), peak[...])
+            ctx[at, lanes] = jnp.where(lane < 64, parts[0], parts[1]).astype(low_type)
+
+    def first_norm(i):
+        at = slice(i * 256, i * 256 + 256)
+        place_of = lax.broadcasted_iota(jnp.int32, (256, 128), 1)
+
+        @pl.loop(0, 4)
+        def _(j):
+            to = pl.ds(pl.multiple_of(j * 256, 256), 256)
+            n1[at, to] = (tokens[at, to] + jnp.dot(ctx[at, :], wholes[3][:, to], preferred_element_type=jnp.float32)
+                          + full_vec[2:3, to])
+
+        @pl.loop(0, 8)
+        def _(j):
+            some = pl.ds(pl.multiple_of(i * 256 + j * 32, 32), 32)
+            normal, scale = row_stats(n1[some, :])
+            n1[some, :] = normal
+            h1r[some, :] = (normal * full_vec[5:6, :1024] + full_vec[6:7, :1024]).astype(low_type)
+            stat[some, :] = jnp.where(place_of[:32] == H, scale, stat[some, :])
+
+    def hidden(lo, hi):
+        @pl.loop(lo, hi)
+        def _(j):
+            at = pl.ds(pl.multiple_of(j * 256, 256), 256)
+            u = jnp.dot(h1r[...], wholes[4][:, at], preferred_element_type=jnp.float32) + full_vec[3:4, at]
+            below = 0.5 + 0.5 * lax.erf(u * 0.7071067811865476)
+            g[:, at] = (u * below).astype(low_type)
+            gp[:, at] = (below + u * (0.3989422804014327 * jnp.exp(-0.5 * u * u))).astype(low_type)
+
+    def outer_product(step):
+        here = slice(step * 1024, step * 1024 + 1024)
+
+        @pl.loop(0, 4)
+        def _(j):
+            to = pl.ds(pl.multiple_of(j * 256, 256), 256)
+            term = jnp.dot(g[:, here], wholes[5][here, to], preferred_element_type=jnp.float32)
+            if step == 0:
+                output[:, to] = term + (n1[:, to] * full_vec[5:6, to] + full_vec[6:7, to]) + full_vec[4:5, to]
+            else:
+                output[:, to] += term
+
+    def second_norm():
+        sums[...] = jnp.zeros_like(sums)
+
+        @pl.loop(0, tokens_count // 32)
+        def _(i):
+            at = pl.ds(pl.multiple_of(i * 32, 32), 32)
+            normal, scale = row_stats(output[at, :])
+            grad = cotangent[at, :]
+            scaled = grad * full_vec[7:8, :1024]
+            gradient = (scaled - jnp.mean(scaled, axis=-1, keepdims=True)
+                        - normal * jnp.mean(scaled * normal, axis=-1, keepdims=True)) * scale
+            output[at, :] = normal * full_vec[7:8, :1024] + full_vec[8:9, :1024]
+            dz2[at, :] = gradient
+            low = gradient.astype(low_type).astype(jnp.float32)
+            for r, part in enumerate((grad * normal, grad, low)):
+                sums[r * 8 : r * 8 + 8, :] += part.reshape(4, 8, 1024).sum(axis=0)
 
     for e in range(ahead):
         send_own(e)
-    for m in range(count):
-        keep_own(m).start()
     keep_vec = pltpu.make_async_copy(vec, vecs.at[mine], own_vec)
     keep_vec.start()
     items = [(e, step) for e in range(number) for step in range(cols)]
-    for tick in range(len(items) + LAGS[-1]):
-        for lag, stage in zip(LAGS, (z_stage, x_stage, y_stage, c_stage)):
+    last = len(items) + LAGS[2]
+
+    def ready(m):
+        return min((2 * m + 2) * cols + LAGS[2] + 2, last)
+
+    work = [(2, cast_tokens), (4, finish_vectors)]
+    for m, into, bias in ((0, q, 0), (1, k, None), (2, v, 1)):
+        work.append((ready(m), lambda m=m, into=into, bias=bias: (complete(m), project(m, into, bias))))
+    work.append((ready(2), start_attention))
+    work += [(ready(2) + 1 + (2 * pair + half) * cols // 4, lambda pair=pair, half=half: attend(pair, half))
+             for pair in range(H // 2) for half in range(2)]
+    work += [(ready(3), lambda: complete(3)), (ready(3), lambda: first_norm(0)), (ready(3), lambda: first_norm(1))]
+    work.append((ready(4), lambda: complete(4)))
+    work += [(ready(4) + lo // 2, lambda lo=lo: hidden(lo, lo + 2)) for lo in range(0, 16, 2)]
+    work += [(ready(5), lambda: complete(5))] + [(ready(5), lambda s=s: outer_product(s)) for s in range(4)]
+    work.append((ready(5), second_norm))
+
+    for tick in range(last + 1):
+        for lag, stage in zip(LAGS[:3], (z_stage, x_stage, y_stage)):
             if 0 <= tick - lag < len(items):
                 stage(*items[tick - lag])
-    for step in range(1, rows * cols):
-        peer = (mine + step) % (rows * cols)
-        wait_arrival(vecs.at[peer], v_in.at[peer], {"row": peer // cols, "col": peer % cols})
+        while work and (work[0][0] <= tick or tick == last):
+            work.pop(0)[1]()
     for m in range(count):
-        keep_own(m).wait()
-    keep_vec.wait()
+        keep(m).wait()
     sends.finish()
 
 
-def gather_all(blocks, vec, ahead=3):
+def forward_all(blocks, vec, lengths, tokens, cotangent, seg, ahead=3):
     rows, cols = lax.axis_size("row"), lax.axis_size("col")
-    count = len(blocks)
-    wholes = [jax.ShapeDtypeStruct((b.shape[0] * rows, b.shape[1] * cols), b.dtype) for b in blocks]
-    out_shape = (*wholes, jax.ShapeDtypeStruct((rows * cols, *vec.shape), vec.dtype))
+    wholes = [jax.ShapeDtypeStruct((b.shape[0] * rows, b.shape[1] * cols), low_type) for b in blocks]
     entries = entries_of([b.shape[0] for b in blocks])
     number = len(entries)
-    dma = pltpu.SemaphoreType.DMA
-    return pl.pallas_call(
-        functools.partial(gather_kernel, rows, cols, entries, ahead),
-        out_shape=out_shape,
-        in_specs=[pl.BlockSpec(memory_space=pltpu.VMEM)] * (count + 1),
-        out_specs=[pl.BlockSpec(memory_space=pl.ANY)] * (count + 1),
-        scratch_shapes=[
+    dma, vm, count = pltpu.SemaphoreType.DMA, pltpu.VMEM, tokens.shape[0]
+    width, hidden = wholes[4].shape
+    shape = jax.ShapeDtypeStruct
+    f32 = jnp.float32
+    results = [shape((16, hidden), f32), *[shape((count, width), low_type)] * 4, shape((count, 128), f32), shape((8, 128), f32),
+               shape((count, width), f32), shape((count, width), low_type), shape((count, hidden), low_type),
+               shape((count, hidden), low_type), shape((count, width), f32), shape((count, width), f32), shape((24, width), f32)]
+    in_vmem = pl.BlockSpec(memory_space=pltpu.VMEM)
+    found = pl.pallas_call(
+        functools.partial(forward_kernel, rows, cols, entries, lengths, ahead),
+        out_shape=(*wholes, *results),
+        in_specs=[in_vmem] * 11,
+        out_specs=[pl.BlockSpec(memory_space=pl.ANY)] * 6 + [in_vmem] * len(results),
+        scratch_shapes=[vm(w.shape, low_type) for w in wholes] + [
+            vm((rows * cols, *vec.shape), vec.dtype), vm(tokens.shape, low_type),
             dma((number, cols)), dma((number, cols)), dma((number, rows, cols)), dma((number, rows, cols, 2)), dma((rows * cols,)),
             dma((number, cols, 2)), dma((number, cols)), dma((number, rows, cols)), dma((number, rows, cols, 2)), dma((rows * cols,)),
-            dma((count,)), dma,
+            dma((6,)), dma,
         ],
-        compiler_params=pltpu.CompilerParams(collective_id=0, has_side_effects=True),
-        name="gather_all",
-    )(*blocks, vec)
+        compiler_params=pltpu.CompilerParams(collective_id=0, has_side_effects=True, vmem_limit_bytes=65400 * 1024),
+        name="forward_all",
+    )(*blocks, vec, tokens, cotangent, seg.reshape(-1, 1), seg.reshape(1, -1))
+    return found[:6], found[6:]
 
 
 RL = (0, 1, 2, 3, 4, 5, 6)
@@ -466,21 +621,6 @@
     )(*terms, vec)
 
 
-norm_eps = 1e-12
-neg_fill = -1e30
-low_type = jnp.bfloat16
-
-
-def norm_rows(values, gain_vec, shift_vec):
-    center = values - jnp.mean(values, axis=-1, keepdims=True)
-    spread = jnp.mean(center * center, axis=-1, keepdims=True)
-    return center * lax.rsqrt(spread + norm_eps) * gain_vec + shift_vec
-
-
-def gelu_exact(values):
-    return jax.nn.gelu(values, approximate=False)
-
-
 def forward_dot(operand, weight):
     return jnp.dot(operand, weight, preferred_element_type=jnp.float32)
 
@@ -507,6 +647,11 @@
 
 def vector_rows(vectors):
     return jnp.concatenate([v.reshape(-1, 128) for v in vectors])
+
+
+def pad_rows(vector):
+    short = -vector.shape[0] % 128
+    return jnp.pad(vector, (0, short)).reshape(-1, 128)
 
 
 def on_device(tokens, segment_ids, cotangent, weight_query, weight_key, weight_value, weight_output, weight_inner,
@@ -518,56 +663,37 @@
     vectors = (bias_query, bias_value, bias_output, bias_inner, bias_outer, gain_attn, shift_attn, gain_block, shift_block)
     lengths = [v.shape[0] for v in vectors]
     spread = [n * groups for n in lengths]
-    flat = jnp.concatenate(vectors).astype(low_type)
-    vec_rows = -(-flat.shape[0] // 2048) * 16
-    flat = jnp.pad(flat, (0, vec_rows * 128 - flat.shape[0])).reshape(vec_rows, 128)
-    gathered = gather_all([m.astype(low_type) for m in matrices], flat)
-    whole_query, whole_key, whole_value, whole_output, whole_inner, whole_outer = gathered[:6]
-    all_vecs = gathered[6].reshape(groups, -1)
-    full, start = [], 0
-    for n in lengths:
-        full.append(all_vecs[:, start : start + n].reshape(-1).astype(jnp.float32))
-        start += n
-    (add_query, add_value, add_output, add_inner, add_outer,
-     scale_attn, offset_attn, scale_block, offset_block) = full
+    flat = jnp.concatenate([pad_rows(v) for v in vectors]).astype(low_type)
+    flat = jnp.pad(flat, ((0, -flat.shape[0] % 16), (0, 0)))
+    wholes, found = forward_all(matrices, flat, lengths, tokens, cotangent, segment_ids)
+    whole_query, whole_key, whole_value, whole_output, whole_inner, whole_outer = wholes
+    (params, query_low, key_low, value_low, context_low, stat, peak, normal_first, normed_low, activated_low,
+     slope, output, grad_second, sums) = found
+    scale_attn = params[5, : tokens.shape[1]]
+    sums = sums.reshape(3, 8, -1).sum(axis=1)
 
     token_count = tokens.shape[0]
     seq_count = token_count // SEQ
     head_shape = (seq_count, SEQ, H, DH)
     token_low = tokens.astype(low_type)
-    query_low = (forward_dot(token_low, whole_query) + add_query).astype(low_type)
-    key_low = forward_dot(token_low, whole_key).astype(low_type)
-    value_low = (forward_dot(token_low, whole_value) + add_value).astype(low_type)
     query_heads = query_low.reshape(head_shape)
     key_heads = key_low.reshape(head_shape)
     value_heads = value_low.reshape(head_shape)
     segment_rows = segment_ids.reshape(seq_count, SEQ)
     allowed = (segment_rows[:, :, None] == segment_rows[:, None, :])[:, None, :, :]
-    masked = masked_scores(query_heads, key_heads, allowed)
-    local_top = jnp.max(masked, axis=(0, 2, 3))
-    row_top = jnp.max(masked, axis=-1, keepdims=True)
-    raised = jnp.exp(masked - row_top)
-    row_total = jnp.sum(raised, axis=-1, keepdims=True)
-    attend = raised / row_total
-    log_total = row_top + jnp.log(row_total)
-    context = jnp.einsum("shqk,skhd->sqhd", attend.astype(low_type), value_heads, preferred_element_type=jnp.float32)
-    context_low = context.reshape(token_count, H * DH).astype(low_type)
-    first_sum = tokens + forward_dot(context_low, whole_output) + add_output
-    normed = norm_rows(first_sum, scale_attn, offset_attn)
-    normed_low = normed.astype(low_type)
-    hidden_pre = forward_dot(normed_low, whole_inner) + add_inner
-    activated_low = gelu_exact(hidden_pre).astype(low_type)
-    second_sum = normed + forward_dot(activated_low, whole_outer) + add_outer
-    output = norm_rows(second_sum, scale_block, offset_block)
-    grad_second, grad_scale_block, grad_offset_block = jax.vjp(norm_rows, second_sum, scale_block, offset_block)[1](cotangent)
     outer_grad_low = grad_second.astype(low_type)
     act_grad = back_dot(outer_grad_low, whole_outer)
-    hidden_grad_low = jax.vjp(gelu_exact, hidden_pre)[1](act_grad)[0].astype(low_type)
+    hidden_grad_low = (act_grad * slope.astype(jnp.float32)).astype(low_type)
     normed_grad = grad_second + back_dot(hidden_grad_low, whole_inner)
-    grad_first, grad_scale_attn, grad_offset_attn = jax.vjp(norm_rows, first_sum, scale_attn, offset_attn)[1](normed_grad)
+    scaled = normed_grad * scale_attn
+    grad_first = (scaled - jnp.mean(scaled, axis=-1, keepdims=True)
+                  - normal_first * jnp.mean(scaled * normal_first, axis=-1, keepdims=True)) * stat[:, H : H + 1]
+    grad_scale_attn = jnp.sum(normed_grad * normal_first, axis=0)
+    grad_offset_attn = jnp.sum(normed_grad, axis=0)
     branch_grad_low = grad_first.astype(low_type)
     context_grad_low = back_dot(branch_grad_low, whole_output).astype(low_type)
     masked_again = masked_scores(query_heads, key_heads, allowed)
+    log_total = stat[:, :H].T[None, :, :, None]
     attend_again = jnp.exp(masked_again - log_total)
     attend_low = attend_again.astype(low_type)
     context_grad_heads = context_grad_low.reshape(head_shape)
@@ -591,10 +717,8 @@
         weight_term(activated_low, outer_grad_low),
     )
     vector_grads = (column_sum(query_grad_low), column_sum(value_grad_low), column_sum(branch_grad_low),
-                    column_sum(hidden_grad_low), column_sum(outer_grad_low),
-                    grad_scale_attn, grad_offset_attn, grad_scale_block, grad_offset_block)
-    peak_rows = jnp.pad(local_top, (0, 1024 - H), constant_values=neg_fill)
-    vec = vector_rows((*vector_grads, peak_rows))
+                    column_sum(hidden_grad_low), sums[2], grad_scale_attn, grad_offset_attn, sums[0], sums[1])
+    vec = vector_rows((*vector_grads, peak))
     reduced = reduce_all(terms, vec, (5, 4, 3, 0, 1, 2))
     block_grads, vec_total = sum_groups(reduced[:6], reduced[6])
 

time: 517 us -> 491 us (0.950); the launches traced: 514 us -> 482 us
  matrix products: 144 us -> 96.2 us
  Pallas kernels: 300 us -> 336 us
  other arithmetic: 38 us -> 19.8 us
    dot_general x7 -> x0, matrix products: 48.5 us -> none  [the longest x6 40.8 us: forward_dot(): return jnp.dot(operand, weight, preferred_element_type=jnp.float32)]
    pallas_call x1, Pallas kernels: 130 us -> 160 us  [forward_all(): pl.pallas_call(functools.partial(forward_kernel, rows, cols, entries, len...]
    reduce_sum x6 -> x1, other arithmetic: 13.2 us -> 0.04 us  [on_device(): sums = sums.reshape(3, 8, -1).sum(axis=1)]
    convert_element_type x8 -> x0, other arithmetic: 9.66 us -> none  [the longest x6 9.5 us: on_device(): gathered = gather_all([m.astype(low_type) for m in matrices], flat)]
    unnamed x161 -> x94, local copies, waits for them, and re-layouts: 20.1 us -> 11.9 us
    dot_general x1, matrix products: 14.7 us -> 8.19 us  [on_device(): jnp.einsum('sqhd,skhd->shqk', context_grad_heads, value_heads, preferred_...]
    pallas_call x1, Pallas kernels: 170 us -> 176 us  [reduce_all(): pl.pallas_call(functools.partial(reduce_kernel, rows, cols, entries), out...]
where the time goes in v2:
time: 491 us; the launch traced here: 482 us
  Pallas kernels  336 us (68%)
  matrix products  96.2 us (20%)
  local copies, waits for them, and re-layouts  27.5 us (6%)
  other arithmetic  19.8 us (4%)
    pallas_call x1, Pallas kernels, reduce_all(): pl.pallas_call(functools.partial(reduce_kernel, rows, cols, entries), out...  176 us
    pallas_call x1, Pallas kernels, forward_all(): pl.pallas_call(functools.partial(forward_kernel, rows, cols, entries, len...  160 us
    dot_general x6, matrix products, back_dot(): lax.dot_general(gradient, weight, (((1,), (1,)), ((), ())), preferred_ele...  36.6 us
    dot_general x6, matrix products, weight_term(): lax.dot_general(operand, gradient, (((0,), (0,)), ((), ())), preferred_el...  26.6 us
    dot_general x1, matrix products, masked_scores(): jnp.einsum('sqhd,skhd->shqk', query_heads, key_heads, preferred_element_t...  12 us
    convert_element_type x1, other arithmetic, on_device(): score_grad_low = score_grad.astype(low_type)  12 us
    unnamed x94, local copies, waits for them, and re-layouts  11.9 us

profile of v2, /device:TPU:5, one launch (start us, length us, event | category | flops | bytes accessed | tf_op | source)
XLA Modules:
  0.0 481.9 jit_solution(13587781344081317633)
XLA Ops:
  0.7 0.7 convert_bitcast_fusion.10
  1.3 0.7 convert_bitcast_fusion.8
  2.0 0.7 convert_bitcast_fusion.3
  2.7 0.7 convert_bitcast_fusion.6
  3.4 0.7 convert_bitcast_fusion.4
  4.7 1.5 copy.66.refs_9_
  6.2 160.2 %forward_all.1 = (bf16[1024,1024]{1,0:T(8,128)(2,1)}, bf16[1024,1024]{1,0:T(8,128)(2,1)}, bf16[1024,1024]{1,0:T(8,128)(2,1)}, bf16[1024,1024]{1,0:T(8,128)(2,1)}...) custom-call(f32[512,256]{1,0:T(8,128)} %refs_0_.1, ...), custom_call_target="tpu_custom_call" | custom-call | tf_op jit(solution)/shard_map/forward_all/pallas_call | solution.py:370
  166.5 1.7 copy.68
  168.4 0.8 slice.48
  169.2 12.4 %convert_reduce_fusion = (f32[4096]{0:T(1024)}, bf16[512,4096]{1,0:T(8,128)(2,1)}) fusion(bf16[512,4096]{1,0:T(8,128)(2,1)} %get-tuple-element.50, bf16[4096,1024]{1,0:T(8,128)(2,1)} %get-tuple-element.49, f32[512,1024]{1,0:T(8,128)} %get-tuple-element.48), kind=kOutput, calls=%fused_computation.3 | convolution fusion | flops 4305973248 | bytes 18890752 | tf_op jit(solution)/shard_map/dot_general | solution.py:629
  181.6 9.5 %multiply_reduce_fusion.1 = (f32[1024]{0:T(1024)}, f32[512]{0:T(512)S(1)}, f32[512]{0:T(512)S(1)}, f32[1024]{0:T(1024)}, f32[512,1024]{1,0:T(8,128)S(1)}) fusion(f32[512,1024]{1,0:T(8,128)S(1)} %copy-done.7, f32[1024]{0:T(1024)S(1)} %bitcast.127, f32[512,1024]{1,0:T(8,128)S(1)} %copy-done.27, bf16[512,4096]{1,0:T(8,128)(2,1)} %get-tuple-element.103, ...), kind=kOutput, calls=%fused_computation.9 | convolution fusion | flops 4299158528 | bytes 18890752 | tf_op jit(solution)/shard_map/dot_general | solution.py:629
  191.1 1.8 convert_reduce_fusion.1
  193.0 2.9 convolution_convert_fusion.3
  196.4 1.5 copy.71
  197.9 8.2 %fusion.13 = f32[16,512,512]{1,2,0:T(8,128)} fusion(bf16[512,16,64]{0,2,1:T(8,128)(2,1)S(1)} %bitcast.116, bf16[512,16,64]{0,2,1:T(8,128)(2,1)S(1)} %bitcast.118), kind=kOutput, calls=%fused_computation.78 | convolution fusion | flops 536870912 | bytes 18874368 | tf_op jit(solution)/shard_map/sqhd,skhd->shqk/dot_general | solution.py:701
  206.2 1.5 copy.67
  208.0 12.0 %multiply_reduce_fusion = (f32[16,512]{1,0:T(8,128)S(1)}, f32[16,512,512]{1,2,0:T(8,128)}) fusion(f32[16,512,512]{1,2,0:T(8,128)} %fusion.13, f32[16,512]{1,0:T(8,128)S(1)} %copy.69, bf16[512,16,64]{0,2,1:T(8,128)(2,1)S(1)} %bitcast.114, bf16[512,16,64]{0,2,1:T(8,128)(2,1)S(1)} %bitcast.112, pred[512,512]{0,1:T(8,128)(4,1)S(1)} %broadcast_compare_fusion), kind=kOutput, calls=%fused_computation.1 | convolution fusion | flops 557834240 | bytes 35979264 | tf_op jit(solution)/shard_map/sqhd,skhd->shqk/dot_general | solution.py:642
  220.0 12.0 %multiply_convert_fusion = bf16[16,512,512]{1,2,0:T(8,128)(2,1)S(1)} fusion(f32[16,512,512]{1,2,0:T(8,128)} %get-tuple-element.97, f32[16,512,512]{1,2,0:T(8,128)} %fusion.13, f32[16,512]{1,0:T(8,128)S(1)} %get-tuple-element.96), kind=kLoop, calls=%fused_computation | loop fusion | flops 12582912 | bytes 41975808 | tf_op jit(solution)/shard_map/convert_element_type | solution.py:703
  232.0 2.6 multiply_convert_fusion.2
  234.7 0.9 copy-done
  235.5 1.0 copy-done.11
  236.5 2.6 fusion.15
  239.2 5.9 %convert_reduce_fusion.3 = (f32[16,64]{1,0:T(8,128)S(1)}, bf16[16,64,512]{2,1,0:T(8,128)(2,1)S(1)}) fusion(bf16[512,16,64]{0,2,1:T(8,128)(2,1)S(1)} %bitcast.113, bf16[16,512,512]{1,2,0:T(8,128)(2,1)} %copy-done), kind=kOutput, calls=%fused_computation.12 | convolution fusion | flops 538967040 | bytes 10489856 | tf_op jit(solution)/shard_map/shqk,skhd->sqhd/dot_general | solution.py:704
  245.1 1.0 copy-done.2
  246.0 2.6 fusion.14
  248.7 4.3 convert_reduce_fusion.2
  253.0 6.6 %add_add_fusion = f32[512,1024]{1,0:T(8,128)} fusion(f32[512,1024]{1,0:T(8,128)} %fusion.15, f32[512,1024]{1,0:T(8,128)} %get-tuple-element.79, f32[512,1024]{1,0:T(8,128)} %fusion.14, bf16[512,1024]{0,1:T(8,128)(2,1)} %bitcast.119, bf16[1024,1024]{1,0:T(8,128)(2,1)} %get-tuple-element.61), kind=kOutput, calls=%fused_computation.16 | convolution fusion | flops 1075314688 | bytes 11534336 | tf_op jit(solution)/shard_map/dot_general | solution.py:629
  259.5 2.6 convert_bitcast_fusion.2.refs_0_
  262.2 2.6 convert_bitcast_fusion.1.refs_1_
  264.8 2.7 convert_bitcast_fusion.refs_2_
  267.5 4.5 convolution_convert_fusion.2.refs_3_
  272.0 6.9 %convolution_convert_fusion.1.refs_4_ = bf16[1024,4096]{1,0:T(8,128)(2,1)} fusion(bf16[512,1024]{1,0:T(8,128)(2,1)S(1)} %copy-done.32, bf16[512,4096]{1,0:T(8,128)(2,1)S(1)} %copy-done.34), kind=kOutput, calls=%fused_computation.8 | convolution fusion | flops 4299161600 | bytes 13631488 | tf_op jit(solution)/shard_map/dot_general | solution.py:633
  279.0 7.2 %convolution_convert_fusion.refs_5_ = bf16[4096,1024]{1,0:T(8,128)(2,1)} fusion(bf16[512,4096]{1,0:T(8,128)(2,1)S(1)} %copy-done.26, f32[512,1024]{1,0:T(8,128)S(1)} %copy-done.28), kind=kOutput, calls=%fused_computation.7 | convolution fusion | flops 4299685888 | bytes 14680064 | tf_op jit(solution)/shard_map/dot_general | solution.py:633
  286.6 0.6 copy-done.19
  287.2 175.7 %reduce_all.1 = (f32[512,256]{1,0:T(8,128)}, f32[512,256]{1,0:T(8,128)}, f32[512,256]{1,0:T(8,128)}, f32[512,256]{1,0:T(8,128)}, f32[512,1024]{1,0:T(8,128)}, /*index=5*/f32[2048,256]{1,0:T(8,128)}, f32[104,128]{1,0:T(8,128)}) custom-call(bf16[1024,1024]{1,0:T(8,128)(2,1)} %convert_bitcast_fusion.2.refs_0_, ...), custom_call_target="tpu_custom_call" | custom-call | tf_op jit(solution)/shard_map/reduce_all/pallas_call | solution.py:613
  462.9 0.9 slice_bitcast_fusion.2
  465.5 0.7 slice_bitcast_fusion.1
  466.2 0.7 dynamic_slice.30
  471.1 1.2 sqrt_bitcast_fusion
  472.4 1.0 broadcast_multiply_fusion
  473.5 1.3 copy.102
  474.8 0.8 copy.103
  475.6 0.8 copy.104
  476.4 0.8 copy.105
  477.2 0.8 copy.106
  478.0 1.3 copy.107
  479.3 1.0 copy-done.5
  480.4 1.3 copy.108
  (107 shorter events, 7.0 us)
Async XLA Ops:
  166.5 1.7 copy-start.13
  169.2 12.4 %copy-start.7 = (f32[512,1024]{1,0:T(8,128)S(1)}, f32[512,1024]{1,0:T(8,128)}, u32[]{:S(2)}) copy-start(f32[512,1024]{1,0:T(8,128)} %get-tuple-element.53) | copy-start | bytes 6291460
  169.2 12.4 %copy-start.27 = (f32[512,1024]{1,0:T(8,128)S(1)}, f32[512,1024]{1,0:T(8,128)}, u32[]{:S(2)}) copy-start(f32[512,1024]{1,0:T(8,128)} %get-tuple-element.48) | copy-start | bytes 6291460
  191.1 1.9 copy-start.31
  206.1 1.6 copy-start.21
  232.0 3.5 copy-start
  232.0 4.5 copy-start.30
  235.5 1.0 copy-start.11
  236.5 12.1 %slice-start = ((s8[16777216]{0:T(1024)(128)(4,1)}), s8[4194304]{0:T(1024)(128)(4,1)S(1)}, s32[]{:S(2)}) async-start(s8[16777216]{0:T(1024)(128)(4,1)} %bitcast.110), calls=%async_computation | async-start | bytes 8388608
  236.5 12.1 %slice-start.1 = ((s8[16777216]{0:T(1024)(128)(4,1)}), s8[4194304]{0:T(1024)(128)(4,1)S(1)}, s32[]{:S(2)}) async-start(s8[16777216]{0:T(1024)(128)(4,1)} %bitcast.110), calls=%async_computation.1 | async-start | bytes 8388608
  239.2 6.9 %copy-start.29 = (bf16[1024,1024]{1,0:T(8,128)(2,1)S(1)}, bf16[1024,1024]{1,0:T(8,128)(2,1)}, u32[]{:S(2)}) copy-start(bf16[1024,1024]{1,0:T(8,128)(2,1)} %get-tuple-element.59) | copy-start | bytes 6291460
  239.2 9.5 %slice-start.2 = ((s8[16777216]{0:T(1024)(128)(4,1)}), s8[4194304]{0:T(1024)(128)(4,1)S(1)}, s32[]{:S(2)}) async-start(s8[16777216]{0:T(1024)(128)(4,1)} %bitcast.110), calls=%async_computation.2 | async-start | bytes 8388608
  245.1 1.0 copy-start.2
  246.0 2.6 slice-start.3
  252.9 6.6 %copy-start.3 = (bf16[16,64,512]{2,1,0:T(8,128)(2,1)S(1)}, bf16[16,64,512]{2,1,0:T(8,128)(2,1)}, u32[]{:S(2)}) copy-start(bf16[16,64,512]{2,1,0:T(8,128)(2,1)} %copy-done.2) | copy-start | bytes 3145732
  253.0 6.6 %copy-start.10 = (f32[512,1024]{1,0:T(8,128)S(1)}, f32[512,1024]{1,0:T(8,128)}, u32[]{:S(2)}) copy-start(f32[512,1024]{1,0:T(8,128)} %refs_7_.1) | copy-start | bytes 6291460
  259.5 2.6 copy-start.12
  262.1 2.7 copy-start.1
  264.8 2.7 copy-start.33
  267.5 4.6 copy-start.32
  267.5 4.6 copy-start.34
  272.0 6.9 %copy-start.26 = (bf16[512,4096]{1,0:T(8,128)(2,1)S(1)}, bf16[512,4096]{1,0:T(8,128)(2,1)}, u32[]{:S(2)}) copy-start(bf16[512,4096]{1,0:T(8,128)(2,1)} %get-tuple-element.64) | copy-start | bytes 12582916
  272.0 6.9 %copy-start.28 = (f32[512,1024]{1,0:T(8,128)S(1)}, f32[512,1024]{1,0:T(8,128)}, u32[]{:S(2)}) copy-start(f32[512,1024]{1,0:T(8,128)} %get-tuple-element.48) | copy-start | bytes 6291460
  279.0 7.3 %copy-start.20 = (f32[16,64]{1,0:T(8,128)S(1)}, f32[16,64]{1,0:T(8,128)}, u32[]{:S(2)}) copy-start(f32[16,64]{1,0:T(8,128)} %get-tuple-element.100) | copy-start | bytes 12292
  279.0 7.4 %copy-start.22 = (f32[4096]{0:T(1024)S(1)}, f32[4096]{0:T(1024)}, u32[]{:S(2)}) copy-start(f32[4096]{0:T(1024)} %get-tuple-element.102) | copy-start | bytes 49156
  279.0 7.4 %copy-start.18 = (f32[24,1024]{1,0:T(8,128)S(1)}, f32[24,1024]{1,0:T(8,128)}, u32[]{:S(2)}) copy-start(f32[24,1024]{1,0:T(8,128)} %get-tuple-element.65) | copy-start | bytes 294916
  279.0 7.5 %copy-start.25 = (f32[1024]{0:T(1024)S(1)}, f32[1024]{0:T(1024)}, u32[]{:S(2)}) copy-start(f32[1024]{0:T(1024)} %get-tuple-element.74) | copy-start | bytes 12292
  279.0 7.5 %copy-start.24 = (f32[1024]{0:T(1024)S(1)}, f32[1024]{0:T(1024)}, u32[]{:S(2)}) copy-start(f32[1024]{0:T(1024)} %get-tuple-element.77) | copy-start | bytes 12292
  279.0 7.5 %copy-start.23 = (f32[8,128]{1,0:T(8,128)S(1)}, f32[8,128]{1,0:T(8,128)}, u32[]{:S(2)}) copy-start(f32[8,128]{1,0:T(8,128)} %get-tuple-element.66) | copy-start | bytes 12292
  286.5 0.6 copy-start.19
  287.2 185.2 %copy-start.8 = (f32[512,256]{1,0:T(8,128)S(1)}, f32[512,256]{1,0:T(8,128)}, u32[]{:S(2)}) copy-start(f32[512,256]{1,0:T(8,128)} %refs_0_.1) | copy-start | bytes 1572868
  287.2 185.2 %copy-start.9 = (f32[512,256]{1,0:T(8,128)S(1)}, f32[512,256]{1,0:T(8,128)}, u32[]{:S(2)}) copy-start(f32[512,256]{1,0:T(8,128)} %refs_1_.1) | copy-start | bytes 1572868
  462.9 10.6 %copy-start.4 = (f32[512,1024]{1,0:T(8,128)S(1)}, f32[512,1024]{1,0:T(8,128)}, u32[]{:S(2)}) copy-start(f32[512,1024]{1,0:T(8,128)} %get-tuple-element.132) | copy-start | bytes 6291460
  473.4 1.4 copy-start.17
  473.4 2.2 copy-start.16
  473.4 3.0 copy-start.15
  474.8 2.4 copy-start.14
  474.8 3.2 copy-start.6
  478.0 2.3 copy-start.5
